TPU v7x, 32 devices: a whole 2x2x4 slice. The times are simulated.
32 devices in a mesh: ctx: 8 (over z, core), fsdp: 4 (over y, x).
Axes of the slice: x: 2, y: 2, z: 4, core: 2. Of those that a mesh axis runs over, the one named last changes fastest.
Arguments:
- tokens: bfloat16 [4, 1024, 2048], P('fsdp', 'ctx'), may hold values from -6 to 6
- cotangent: bfloat16 [4, 1024, 2048], P('fsdp', 'ctx'), may hold values from -6 to 6
- lengths: int32 [4, 4], P('fsdp'), may hold values from 1 to 768, 1024 in all within a row
- span_order: int32 [4, 16], P('fsdp'), may hold values from 0 to 15, each once within a row
- gain_attn: bfloat16 [2048], P('fsdp'), may hold values from 0.5 to 1.5
- w_query: bfloat16 [2048, 2048], P('fsdp'), may hold values from -0.1875 to 0.1875
- w_key: bfloat16 [2048, 256], P('fsdp'), may hold values from -0.1875 to 0.1875
- w_value: bfloat16 [2048, 256], P('fsdp'), may hold values from -0.125 to 0.125
- w_out: bfloat16 [2048, 2048], P('fsdp'), may hold values from -0.5 to 0.5
- gain_ffn: bfloat16 [2048], P('fsdp'), may hold values from 0.5 to 1.5
- w_gate: bfloat16 [2048, 5632], P('fsdp'), may hold values from -0.125 to 0.125
- w_up: bfloat16 [2048, 5632], P('fsdp'), may hold values from -0.125 to 0.125
- w_down: bfloat16 [5632, 2048], P('fsdp'), may hold values from -0.078125 to 0.078125
Outputs:
- output: bfloat16 [4, 1024, 2048], P('fsdp', 'ctx')
- grad_tokens: bfloat16 [4, 1024, 2048], P('fsdp', 'ctx')
- grad_gain_attn: float32 [2048], P(('ctx', 'fsdp'))
- grad_query: float32 [2048, 2048], P(('ctx', 'fsdp'))
- grad_key: float32 [2048, 256], P(('ctx', 'fsdp'))
- grad_value: float32 [2048, 256], P(('ctx', 'fsdp'))
- grad_out: float32 [2048, 2048], P(('ctx', 'fsdp'))
- grad_gain_ffn: float32 [2048], P(('ctx', 'fsdp'))
- grad_gate: float32 [2048, 5632], P(('ctx', 'fsdp'))
- grad_up: float32 [2048, 5632], P(('ctx', 'fsdp'))
- grad_down: float32 [5632, 2048], P(('ctx', 'fsdp'))
Inputs may be any that keep to these rules, and one draw needn't show every extreme that they name: `lengths`: each row sums to 1024, and its largest entry is exactly 768. `span_order`: each row is a permutation of the 16 spans of its pack.
All inputs are finite; a program needn't handle non-finite values.
Results may differ from a plain program's by a relative error of at most 0.015.
Values may be sent and summed in bfloat16 or wider, within the bound.
No kernel may reach another device: no remote copies, remote signals or barrier semaphores. Data moves between devices by JAX's collectives and lax.ppermute only.
A program may use at most 384 MiB of HBM per device.

v0:
```python
import math

import jax
import jax.numpy as jnp
from jax import lax
from jax.sharding import PartitionSpec as P

HEADS = 32
KV_HEADS = 4
HEAD = 64


EPS = 1e-05
THETA = 10000.0
NEGATIVE = -1e30


def rms_scale(values):
    return lax.rsqrt(jnp.mean(values * values, axis=-1, keepdims=True) + EPS)


def norm_back(values, scale_inv, gain, gradient):
    weighted = gradient * gain
    inner = jnp.mean(weighted * values, axis=-1, keepdims=True)
    return (
        scale_inv * weighted - values * scale_inv * scale_inv * scale_inv * inner,
        jnp.sum(gradient * values * scale_inv, axis=0),
    )


def back_dot(left, weight):
    return lax.dot_general(
        left, weight, (((1,), (1,)), ((), ())), preferred_element_type=jnp.float32
    )


def token_meta(first_row, row_count, seq_ends, seq_starts, dealt_order, span_rows):
    row_ids = first_row + jnp.arange(row_count, dtype=jnp.int32)
    slot_ids = row_ids // span_rows
    slot_table = jnp.arange(dealt_order.shape[0], dtype=jnp.int32)
    chosen = jnp.sum(
        jnp.where(slot_ids[:, None] == slot_table[None, :], dealt_order[None, :], 0), axis=1
    )
    anchor = chosen * span_rows + row_ids % span_rows
    segment = jnp.sum((anchor[:, None] >= seq_ends[None, :]).astype(jnp.int32), axis=1)
    seq_table = jnp.arange(seq_ends.shape[0], dtype=jnp.int32)
    seq_first = jnp.sum(
        jnp.where(segment[:, None] == seq_table[None, :], seq_starts[None, :], 0), axis=1
    )
    return (anchor - seq_first, segment)


def permitted(query_pos, query_seg, key_pos, key_seg):
    return (query_seg[:, None] == key_seg[None, :]) & (key_pos[None, :] <= query_pos[:, None])


def rope_tables(positions):
    half_dim = HEAD // 2
    inverse = THETA ** (-(jnp.arange(half_dim, dtype=jnp.float32) * 2.0 / HEAD))
    angles = positions.astype(jnp.float32)[:, None] * inverse[None, :]
    return (jnp.cos(angles)[:, None, :], jnp.sin(angles)[:, None, :])


def rotate(values, cosine, sine_table):
    half_dim = values.shape[-1] // 2
    front_half, back_half = (values[..., :half_dim], values[..., half_dim:])
    return jnp.concatenate(
        [
            front_half * cosine - back_half * sine_table,
            back_half * cosine + front_half * sine_table,
        ],
        axis=-1,
    )


def rotate_back(gradient, cosine, sine_table):
    half_dim = gradient.shape[-1] // 2
    front_half, back_half = (gradient[..., :half_dim], gradient[..., half_dim:])
    return jnp.concatenate(
        [
            front_half * cosine + back_half * sine_table,
            back_half * cosine - front_half * sine_table,
        ],
        axis=-1,
    )


def over_blocks(step_fn, running, pieces, max_rows):
    piece_rows = pieces[0].shape[0]
    block_count = piece_rows // max_rows
    block_rows = piece_rows // block_count

    def advance(state, block_index):
        sliced = tuple(
            (
                lax.dynamic_slice_in_dim(member, block_index * block_rows, block_rows, 0)
                for member in pieces
            )
        )
        return (step_fn(state, sliced, block_index * block_rows), None)

    running, _ = lax.scan(advance, running, jnp.arange(block_count, dtype=jnp.int32))
    return running


def weight_term(left, right):
    return lax.dot_general(
        left, right, (((0,), (0,)), ((), ())), preferred_element_type=jnp.float32
    )


def reduce_pack(left, right):
    return lax.psum_scatter(weight_term(left, right), "ctx", scatter_dimension=0, tiled=True)


def on_device(
    tokens,
    cotangent,
    lengths,
    span_order,
    gain_attn,
    w_query,
    w_key,
    w_value,
    w_out,
    gain_ffn,
    w_gate,
    w_up,
    w_down,
):
    tok_rows = tokens.shape[1]
    span_rows = tok_rows // 2
    group_heads = HEADS // KV_HEADS
    score_scale = 1.0 / math.sqrt(HEAD)
    seq_ends = jnp.cumsum(lengths[0])
    seq_starts = seq_ends - lengths[0]
    dealt = span_order[0]

    def meta_of(first_row, row_count):
        return token_meta(first_row, row_count, seq_ends, seq_starts, dealt, span_rows)

    my_pos, my_seg = meta_of(lax.axis_index("ctx") * tok_rows, tok_rows)
    cosine, sine_table = rope_tables(my_pos)
    gathered = (
        lax.all_gather(gain_attn, "fsdp", axis=0, tiled=True),
        lax.all_gather(w_query, "fsdp", axis=0, tiled=True),
        lax.all_gather(w_key, "fsdp", axis=0, tiled=True),
        lax.all_gather(w_value, "fsdp", axis=0, tiled=True),
        lax.all_gather(w_out, "fsdp", axis=0, tiled=True),
        lax.all_gather(gain_ffn, "fsdp", axis=0, tiled=True),
        lax.all_gather(w_gate, "fsdp", axis=0, tiled=True),
        lax.all_gather(w_up, "fsdp", axis=0, tiled=True),
        lax.all_gather(w_down, "fsdp", axis=0, tiled=True),
    )
    gain_one, wq_full, wk_full, wv_full, wo_full, gain_two, wg_full, wu_full, wd_full = gathered
    inputs = tokens[0].astype(jnp.float32)
    scale_one = rms_scale(inputs)
    normed_one = (inputs * scale_one * gain_one.astype(jnp.float32)).astype(jnp.bfloat16)
    query_lin = jnp.dot(normed_one, wq_full, preferred_element_type=jnp.float32)
    key_lin = jnp.dot(normed_one, wk_full, preferred_element_type=jnp.float32)
    value_lin = jnp.dot(normed_one, wv_full, preferred_element_type=jnp.float32)
    queries = (
        rotate(query_lin.reshape(tok_rows, HEADS, HEAD), cosine, sine_table)
        .astype(jnp.bfloat16)
        .reshape(tok_rows, KV_HEADS, group_heads, HEAD)
    )
    keys = rotate(key_lin.reshape(tok_rows, KV_HEADS, HEAD), cosine, sine_table).astype(
        jnp.bfloat16
    )
    values = value_lin.astype(jnp.bfloat16).reshape(tok_rows, KV_HEADS, HEAD)

    def query_scores(key_block, first_row):
        key_pos, key_seg = meta_of(first_row, key_block.shape[0])
        allowed = permitted(my_pos, my_seg, key_pos, key_seg)
        raw = jnp.einsum("tkgd,pkd->kgtp", queries, key_block, preferred_element_type=jnp.float32)
        return (jnp.where(allowed[None, None], score_scale * raw, NEGATIVE), allowed)

    def max_step(running, pieces, first_row):
        row_max, row_sum = running
        scores, allowed = query_scores(pieces[0], first_row)
        new_max = jnp.maximum(row_max, jnp.max(scores, axis=-1))
        fresh = jnp.sum(
            jnp.where(allowed[None, None], jnp.exp(scores - new_max[..., None]), 0.0), axis=-1
        )
        return (new_max, row_sum * jnp.exp(row_max - new_max) + fresh)

    stat_shape = (KV_HEADS, group_heads, tok_rows)
    row_max, row_sum = over_blocks(
        max_step,
        (jnp.full(stat_shape, NEGATIVE, jnp.float32), jnp.zeros(stat_shape, jnp.float32)),
        (lax.all_gather(keys, "ctx", axis=0, tiled=True),),
        tok_rows,
    )
    log_norm = row_max + jnp.log(row_sum)

    def value_step(running, pieces, first_row):
        key_block, value_block = pieces
        scores, allowed = query_scores(key_block, first_row)
        weights = jnp.exp(scores - log_norm[..., None]).astype(jnp.bfloat16)
        return running + jnp.einsum(
            "kgtp,pkd->tkgd", weights, value_block, preferred_element_type=jnp.float32
        )

    attn_acc = over_blocks(
        value_step,
        jnp.zeros((tok_rows, KV_HEADS, group_heads, HEAD), jnp.float32),
        (
            lax.all_gather(keys, "ctx", axis=0, tiled=True),
            lax.all_gather(values, "ctx", axis=0, tiled=True),
        ),
        tok_rows,
    )
    attended = attn_acc.reshape(tok_rows, HEADS * HEAD).astype(jnp.bfloat16)
    hidden_in = inputs + jnp.dot(attended, wo_full, preferred_element_type=jnp.float32)
    scale_two = rms_scale(hidden_in)
    normed_two = (hidden_in * scale_two * gain_two.astype(jnp.float32)).astype(jnp.bfloat16)
    gate_lin = jnp.dot(normed_two, wg_full, preferred_element_type=jnp.float32)
    up_lin = jnp.dot(normed_two, wu_full, preferred_element_type=jnp.float32)
    sigmoid_gate = jax.nn.sigmoid(gate_lin)
    activated = (gate_lin * sigmoid_gate * up_lin).astype(jnp.bfloat16)
    result = hidden_in + jnp.dot(activated, wd_full, preferred_element_type=jnp.float32)
    output = result.astype(jnp.bfloat16)[None]
    backward_set = (
        lax.all_gather(gain_attn, "fsdp", axis=0, tiled=True),
        lax.all_gather(w_query, "fsdp", axis=0, tiled=True),
        lax.all_gather(w_key, "fsdp", axis=0, tiled=True),
        lax.all_gather(w_value, "fsdp", axis=0, tiled=True),
        lax.all_gather(w_out, "fsdp", axis=0, tiled=True),
        lax.all_gather(gain_ffn, "fsdp", axis=0, tiled=True),
        lax.all_gather(w_gate, "fsdp", axis=0, tiled=True),
        lax.all_gather(w_up, "fsdp", axis=0, tiled=True),
        lax.all_gather(w_down, "fsdp", axis=0, tiled=True),
    )
    gain_one_b, wq_back, wk_back, wv_back, wo_back, gain_two_b, wg_back, wu_back, wd_back = (
        backward_set
    )
    upstream = cotangent[0]
    act_grad = back_dot(upstream, wd_back)
    gate_grad = (act_grad * up_lin * sigmoid_gate * (1.0 + gate_lin * (1.0 - sigmoid_gate))).astype(
        jnp.bfloat16
    )
    up_grad = (act_grad * gate_lin * sigmoid_gate).astype(jnp.bfloat16)
    norm_two_grad = back_dot(gate_grad, wg_back) + back_dot(up_grad, wu_back)
    hidden_norm_grad, gain_two_grad = norm_back(
        hidden_in, scale_two, gain_two_b.astype(jnp.float32), norm_two_grad
    )
    hidden_grad = upstream.astype(jnp.float32) + hidden_norm_grad
    branch_grad = hidden_grad.astype(jnp.bfloat16)
    attended_grad = (
        back_dot(branch_grad, wo_back)
        .astype(jnp.bfloat16)
        .reshape(tok_rows, KV_HEADS, group_heads, HEAD)
    )
    delta_rows = jnp.sum(attended_grad.astype(jnp.float32) * attn_acc, axis=-1)
    delta_stat = delta_rows.transpose(1, 2, 0)
    log_norm_rows = log_norm.transpose(2, 0, 1)

    def query_grad_step(running, pieces, first_row):
        key_block, value_block = pieces
        scores, allowed = query_scores(key_block, first_row)
        probs = jnp.exp(scores - log_norm[..., None])
        prob_grad = jnp.einsum(
            "tkgd,pkd->kgtp", attended_grad, value_block, preferred_element_type=jnp.float32
        )
        score_grad = (probs * (prob_grad - delta_stat[..., None])).astype(jnp.bfloat16)
        return running + jnp.einsum(
            "kgtp,pkd->tkgd", score_grad, key_block, preferred_element_type=jnp.float32
        )

    query_grad = over_blocks(
        query_grad_step,
        jnp.zeros((tok_rows, KV_HEADS, group_heads, HEAD), jnp.float32),
        (
            lax.all_gather(keys, "ctx", axis=0, tiled=True),
            lax.all_gather(values, "ctx", axis=0, tiled=True),
        ),
        tok_rows,
    )

    def key_grad_step(running, pieces, first_row):
        key_acc, value_acc = running
        query_block, out_grad_block, norm_block, delta_block = pieces
        query_pos, query_seg = meta_of(first_row, query_block.shape[0])
        allowed = permitted(query_pos, query_seg, my_pos, my_seg)
        raw = jnp.einsum("pkgd,tkd->kgpt", query_block, keys, preferred_element_type=jnp.float32)
        scores = jnp.where(allowed[None, None], score_scale * raw, NEGATIVE)
        probs = jnp.exp(scores - norm_block.transpose(1, 2, 0)[..., None])
        value_acc = value_acc + jnp.einsum(
            "kgpt,pkgd->tkd",
            probs.astype(jnp.bfloat16),
            out_grad_block,
            preferred_element_type=jnp.float32,
        )
        prob_grad = jnp.einsum(
            "pkgd,tkd->kgpt", out_grad_block, values, preferred_element_type=jnp.float32
        )
        score_grad = (probs * (prob_grad - delta_block.transpose(1, 2, 0)[..., None])).astype(
            jnp.bfloat16
        )
        key_acc = key_acc + jnp.einsum(
            "kgpt,pkgd->tkd", score_grad, query_block, preferred_element_type=jnp.float32
        )
        return (key_acc, value_acc)

    empty_kv = jnp.zeros((tok_rows, KV_HEADS, HEAD), jnp.float32)
    key_grad, value_grad = over_blocks(
        key_grad_step,
        (empty_kv, empty_kv),
        (
            lax.all_gather(queries.astype(jnp.float32), "ctx", axis=0, tiled=True).astype(
                jnp.bfloat16
            ),
            lax.all_gather(attended_grad.astype(jnp.float32), "ctx", axis=0, tiled=True).astype(
                jnp.bfloat16
            ),
            lax.all_gather(log_norm_rows, "ctx", axis=0, tiled=True),
            lax.all_gather(delta_rows, "ctx", axis=0, tiled=True),
        ),
        tok_rows,
    )
    query_lin_grad = (
        rotate_back(query_grad.reshape(tok_rows, HEADS, HEAD) * score_scale, cosine, sine_table)
        .reshape(tok_rows, HEADS * HEAD)
        .astype(jnp.bfloat16)
    )
    key_lin_grad = (
        rotate_back(key_grad * score_scale, cosine, sine_table)
        .reshape(tok_rows, KV_HEADS * HEAD)
        .astype(jnp.bfloat16)
    )
    value_lin_grad = value_grad.reshape(tok_rows, KV_HEADS * HEAD).astype(jnp.bfloat16)
    norm_one_grad = (
        back_dot(query_lin_grad, wq_back)
        + back_dot(key_lin_grad, wk_back)
        + back_dot(value_lin_grad, wv_back)
    )
    input_norm_grad, gain_one_grad = norm_back(
        inputs, scale_one, gain_one_b.astype(jnp.float32), norm_one_grad
    )
    input_grad = (hidden_grad + input_norm_grad).astype(jnp.bfloat16)[None]
    term_pairs = (
        (normed_one, query_lin_grad),
        (normed_one, key_lin_grad),
        (normed_one, value_lin_grad),
        (attended, branch_grad),
        (normed_two, gate_grad),
        (normed_two, up_grad),
        (activated, upstream),
    )
    gain_terms = jnp.stack([gain_one_grad, gain_two_grad])
    pack_sums = tuple((reduce_pack(left, right) for left, right in term_pairs))
    gain_pack = lax.psum_scatter(gain_terms, "ctx", scatter_dimension=1, tiled=True)
    summed = (
        lax.psum_scatter(pack_sums[0], "fsdp", scatter_dimension=0, tiled=True),
        lax.psum_scatter(pack_sums[1], "fsdp", scatter_dimension=0, tiled=True),
        lax.psum_scatter(pack_sums[2], "fsdp", scatter_dimension=0, tiled=True),
        lax.psum_scatter(pack_sums[3], "fsdp", scatter_dimension=0, tiled=True),
        lax.psum_scatter(pack_sums[4], "fsdp", scatter_dimension=0, tiled=True),
        lax.psum_scatter(pack_sums[5], "fsdp", scatter_dimension=0, tiled=True),
        lax.psum_scatter(pack_sums[6], "fsdp", scatter_dimension=0, tiled=True),
        lax.psum_scatter(gain_pack, "fsdp", scatter_dimension=1, tiled=True),
    )
    grad_mats = summed[:7]
    gain_sums = summed[7]
    return (
        output,
        input_grad,
        gain_sums[0],
        grad_mats[0],
        grad_mats[1],
        grad_mats[2],
        grad_mats[3],
        gain_sums[1],
        grad_mats[4],
        grad_mats[5],
        grad_mats[6],
    )


def solution(mesh):
    in_specs = (
        P("fsdp", "ctx", None),
        P("fsdp", "ctx", None),
        P("fsdp", None),
        P("fsdp", None),
        P("fsdp"),
        P("fsdp", None),
        P("fsdp", None),
        P("fsdp", None),
        P("fsdp", None),
        P("fsdp"),
        P("fsdp", None),
        P("fsdp", None),
        P("fsdp", None),
    )
    out_specs = (
        P("fsdp", "ctx", None),
        P("fsdp", "ctx", None),
        P(("ctx", "fsdp")),
        P(("ctx", "fsdp"), None),
        P(("ctx", "fsdp"), None),
        P(("ctx", "fsdp"), None),
        P(("ctx", "fsdp"), None),
        P(("ctx", "fsdp")),
        P(("ctx", "fsdp"), None),
        P(("ctx", "fsdp"), None),
        P(("ctx", "fsdp"), None),
    )
    return jax.shard_map(
        on_device, mesh=mesh, in_specs=in_specs, out_specs=out_specs, check_vma=False
    )
```

profile of v0, /device:TPU:0, one launch (start us, length us, event | category | flops | bytes accessed | tf_op | source)
XLA Modules:
  0.0 3265.7 jit_solution(16975288538213545888)
XLA Ops:
  12.1 9.6 all-gather
  22.4 8.1 all-gather.1
  34.8 4.3 all-gather.12.cloned.1.call-done
  40.8 26.7 all-gather.14.cloned.1.call-done
  69.5 14.7 all_gather.59
  84.2 14.7 all_gather.61
  98.9 57.9 %all-gather.16.cloned.1.call-done = bf16[2048,2048]{1,0:T(8,128)(2,1)} async-done(((bf16[512,2048]{1,0:T(8,128)(2,1)}), bf16[2048,2048]{1,0:T(8,128)(2,1)}) %all-gather.16.cloned.1.call-update) | async-done | bytes 8388624 | tf_op jit(solution)/shard_map/all_gather | solution.py:146
  156.8 12.4 copy.51
  169.2 6.2 fusion.103
  176.2 49.3 %while.56 = (s32[]{:T(128)}, f32[4,8,128]{2,1,0:T(8,128)S(1)}, f32[4,8,128]{2,1,0:T(8,128)S(1)}, s32[128]{0:T(128)S(1)}, s32[8]{0:T(128)}, /*index=5*/s32[1,16]{...) while((s32[]{:T(128)}, f32[4,8,128]{2,1,0:T(8,128)S(1)}, ...), condition=%wide.region_11.12_spmd.clone, body=%wide.region_5.11_spmd.clone.sunk | while | flops 71387400 | bytes 5054794 | solution.py:102
  225.5 53.7 %while.57 = (s32[]{:T(128)}, f32[128,4,8,64]{0,3,2,1:T(8,128)}, s32[8]{0:T(128)S(1)}, bf16[1024,4,64]{0,2,1:T(8,128)(2,1)}, s32[128]{0:T(128)S(1)}, /*index=5*/s...) while((s32[]{:T(128)}, f32[128,4,8,64]{0,3,2,1:T(8,128)}, ...), condition=%wide.region_16.17_spmd.clone, body=%wide.region_12.16_spmd.clone.sunk | while | flops 136902912 | bytes 2811724 | solution.py:102
  229.0 2.7 fusion.216
  235.3 3.1 fusion.216
  241.9 3.1 fusion.216
  248.6 3.1 fusion.216
  255.3 3.6 fusion.216
  262.4 3.4 fusion.216
  269.4 3.1 fusion.216
  276.0 3.1 fusion.216
  280.7 4.9 multiply_reduce_fusion.3
  285.7 15.6 all_gather.69
  301.5 156.6 %all-gather.20.cloned.1.call-done = bf16[2048,5632]{1,0:T(8,128)(2,1)} async-done(((bf16[512,5632]{1,0:T(8,128)(2,1)}), bf16[2048,5632]{1,0:T(8,128)(2,1)}) %all-gather.20.cloned.1.call-update) | async-done | bytes 23068688 | tf_op jit(solution)/shard_map/all_gather | solution.py:151
  458.1 12.5 fusion.128
  470.6 199.5 %all-gather.22.cloned.1.call-done = bf16[2048,5632]{1,0:T(8,128)(2,1)} async-done(((bf16[512,5632]{1,0:T(8,128)(2,1)}), bf16[2048,5632]{1,0:T(8,128)(2,1)}) %all-gather.22.cloned.1.call-update) | async-done | bytes 23068688 | tf_op jit(solution)/shard_map/all_gather | solution.py:152
  670.2 12.6 fusion.129
  682.8 199.6 %all-gather.24.cloned.1.call-done = bf16[5632,2048]{1,0:T(8,128)(2,1)} async-done(((bf16[1408,2048]{1,0:T(8,128)(2,1)}), bf16[5632,2048]{1,0:T(8,128)(2,1)}) %all-gather.24.cloned.1.call-update) | async-done | bytes 23068688 | tf_op jit(solution)/shard_map/all_gather | solution.py:153
  882.4 15.1 multiply_convert_fusion
  897.5 12.3 fusion.130
  909.8 13.8 multiply_reduce_fusion
  925.2 6.7 convolution_convert_fusion
  934.5 71.4 %while.58 = (s32[]{:T(128)}, f32[128,4,8,64]{0,3,2,1:T(8,128)}, s32[8]{0:T(128)}, bf16[1024,4,64]{0,2,1:T(8,128)(2,1)}, s32[128]{0:T(128)S(1)}, /*index=5*/s32[1...) while((s32[]{:T(128)}, f32[128,4,8,64]{0,3,2,1:T(8,128)}, ...), condition=%wide.region_24.25_spmd.clone, body=%wide.region_20.24_spmd.clone.sunk | while | flops 205060352 | bytes 7612256 | solution.py:102
  940.0 3.1 fusion.225
  948.6 3.4 fusion.225
  957.6 3.5 fusion.225
  966.6 3.4 fusion.225
  975.6 3.5 fusion.225
  984.6 3.4 fusion.225
  993.5 3.4 fusion.225
  1002.5 3.4 fusion.225
  1005.9 15.5 all_gather.71
  1022.9 7.3 fusion.131
  1030.2 80.5 %while.59 = (s32[]{:T(128)}, f32[128,4,64]{0,2,1:T(8,128)S(1)}, f32[128,4,64]{0,2,1:T(8,128)S(1)}, s32[8]{0:T(128)S(1)}, bf16[1024,4,8,64]{0,3,2,1:T(8,128)(2,1)...) while((s32[]{:T(128)}, f32[128,4,64]{0,2,1:T(8,128)S(1)}, ...), condition=%wide.region_29.30_spmd.clone, body=%wide.region_25.29_spmd.clone.sunk | while | flops 272300288 | bytes 9185449 | solution.py:102
  1036.6 2.3 fusion.236
  1097.0 2.3 fusion.236
  1119.9 8.3 fusion.107
  1129.6 8.2 fusion.115
  1138.8 19.4 fusion.132
  1158.2 19.5 fusion.133
  1178.8 19.4 fusion.99
  1199.7 22.5 reduce-scatter.29.cloned.1.call-done
  1222.3 169.1 %reduce-scatter.21.cloned.1.call-done = f32[256,2048]{1,0:T(8,128)} async-done(((f32[2048,2048]{1,0:T(8,128)}), f32[256,2048]{1,0:T(8,128)}) %reduce-scatter.21.cloned.1.call-update) | async-done | bytes 2097168 | tf_op jit(solution)/shard_map/reduce_scatter | solution.py:113
  1391.4 168.8 %reduce-scatter.33.cloned.1.call-done = f32[256,2048]{1,0:T(8,128)} async-done(((f32[2048,2048]{1,0:T(8,128)}), f32[256,2048]{1,0:T(8,128)}) %reduce-scatter.33.cloned.1.call-update) | async-done | bytes 2097168 | tf_op jit(solution)/shard_map/reduce_scatter | solution.py:113
  1560.3 444.3 %reduce-scatter.37.cloned.1.call-done = f32[256,5632]{1,0:T(8,128)} async-done(((f32[2048,5632]{1,0:T(8,128)}), f32[256,5632]{1,0:T(8,128)}) %reduce-scatter.37.cloned.1.call-update) | async-done | bytes 5767184 | tf_op jit(solution)/shard_map/reduce_scatter | solution.py:113
  2004.7 444.3 %reduce-scatter.41.cloned.1.call-done = f32[256,5632]{1,0:T(8,128)} async-done(((f32[2048,5632]{1,0:T(8,128)}), f32[256,5632]{1,0:T(8,128)}) %reduce-scatter.41.cloned.1.call-update) | async-done | bytes 5767184 | tf_op jit(solution)/shard_map/reduce_scatter | solution.py:113
  2449.5 443.8 %reduce-scatter.45.cloned.1.call-done = f32[704,2048]{1,0:T(8,128)} async-done(((f32[5632,2048]{1,0:T(8,128)}), f32[704,2048]{1,0:T(8,128)}) %reduce-scatter.45.cloned.1.call-update) | async-done | bytes 5767184 | tf_op jit(solution)/shard_map/reduce_scatter | solution.py:113
  2894.6 12.1 fusion.78
  2907.8 10.8 reduce-scatter.51.cloned.1.call-done
  2920.7 25.6 reduce-scatter.27.cloned.1.call-done
  2946.3 27.5 reduce-scatter.31.cloned.1.call-done
  2973.8 38.8 %reduce-scatter.23.cloned.1.call-done = f32[64,2048]{1,0:T(8,128)} async-done(((f32[256,2048]{1,0:T(8,128)}), f32[64,2048]{1,0:T(8,128)}) %reduce-scatter.23.cloned.1.call-update) | async-done | bytes 524304 | tf_op jit(solution)/shard_map/reduce_scatter | solution.py:354
  3012.6 38.8 %reduce-scatter.35.cloned.1.call-done = f32[64,2048]{1,0:T(8,128)} async-done(((f32[256,2048]{1,0:T(8,128)}), f32[64,2048]{1,0:T(8,128)}) %reduce-scatter.35.cloned.1.call-update) | async-done | bytes 524304 | tf_op jit(solution)/shard_map/reduce_scatter | solution.py:357
  3051.3 69.3 %reduce-scatter.39.cloned.1.call-done = f32[64,5632]{1,0:T(8,128)} async-done(((f32[256,5632]{1,0:T(8,128)}), f32[64,5632]{1,0:T(8,128)}) %reduce-scatter.39.cloned.1.call-update) | async-done | bytes 1441808 | tf_op jit(solution)/shard_map/reduce_scatter | solution.py:358
  3120.6 69.1 %reduce-scatter.43.cloned.1.call-done = f32[64,5632]{1,0:T(8,128)} async-done(((f32[256,5632]{1,0:T(8,128)}), f32[64,5632]{1,0:T(8,128)}) %reduce-scatter.43.cloned.1.call-update) | async-done | bytes 1441808 | tf_op jit(solution)/shard_map/reduce_scatter | solution.py:359
  3189.7 69.3 %reduce-scatter.47.cloned.1.call-done = f32[176,2048]{1,0:T(8,128)} async-done(((f32[704,2048]{1,0:T(8,128)}), f32[176,2048]{1,0:T(8,128)}) %reduce-scatter.47.cloned.1.call-update) | async-done | bytes 1441808 | tf_op jit(solution)/shard_map/reduce_scatter | solution.py:360
  (542 shorter events, 215.7 us)
Async XLA Ops:
  7.2 31.9 all-gather.12.cloned.1.call-start
  7.9 59.6 %all-gather.14.cloned.1.call-start = ((), (), s32[]{:S(2)}) async-start(), calls=%async_computation.17 | async-start | bytes 1310720 | tf_op jit(solution)/shard_map/all_gather | solution.py:147
  8.7 148.2 %all-gather.16.cloned.1.call-start = ((), (), s32[]{:S(2)}) async-start(), calls=%async_computation.18 | async-start | bytes 10485760 | tf_op jit(solution)/shard_map/all_gather | solution.py:146
  9.4 271.3 %all-gather.18.cloned.1.call-start = ((), (), s32[]{:S(2)}) async-start(), calls=%async_computation.19 | async-start | bytes 10485760 | tf_op jit(solution)/shard_map/all_gather | solution.py:149
  10.0 448.1 %all-gather.20.cloned.1.call-start = ((), (), s32[]{:S(2)}) async-start(), calls=%async_computation.20 | async-start | bytes 28835840 | tf_op jit(solution)/shard_map/all_gather | solution.py:151
  10.6 659.6 %all-gather.22.cloned.1.call-start = ((), (), s32[]{:S(2)}) async-start(), calls=%async_computation.21 | async-start | bytes 28835840 | tf_op jit(solution)/shard_map/all_gather | solution.py:152
  11.1 10.5 copy-start.29
  11.2 11.2 copy-start.28
  11.2 22.1 copy-start.2
  11.2 871.2 %all-gather.24.cloned.1.call-start = ((), (), s32[]{:S(2)}) async-start(), calls=%async_computation.22 | async-start | bytes 28835840 | tf_op jit(solution)/shard_map/all_gather | solution.py:153
  11.9 1018.3 %all-gather.26.cloned.1.call-start = ((), (), s32[]{:S(2)}) async-start(), calls=%async_computation.23 | async-start | bytes 4718592 | tf_op jit(solution)/shard_map/all_gather | solution.py:310
  33.5 135.7 %copy-start.25 = (f32[128]{0:T(128)}, f32[128]{0:T(128)S(1)}, u32[]{:S(2)}) copy-start(f32[128]{0:T(128)S(1)} %add_rsqrt_fusion.1) | copy-start | bytes 1540
  34.8 140.6 %copy-start.18 = (f32[128,32]{0,1:T(8,128)}, f32[128,32]{0,1:T(8,128)S(1)}, u32[]{:S(2)}) copy-start(f32[128,32]{0,1:T(8,128)S(1)} %get-tuple-element.1039) | copy-start | bytes 49156
  34.8 140.6 %copy-start.20 = (f32[128,32]{0,1:T(8,128)}, f32[128,32]{0,1:T(8,128)S(1)}, u32[]{:S(2)}) copy-start(f32[128,32]{0,1:T(8,128)S(1)} %get-tuple-element.1040) | copy-start | bytes 49156
  69.5 14.7 copy-start.22
  279.1 6.5 copy-start
  280.6 5.0 copy-start.11
  280.7 20.7 copy-start.23
  285.6 638.0 %copy-start.4 = (f32[128,2048]{1,0:T(8,128)}, f32[128,2048]{1,0:T(8,128)S(1)}, u32[]{:S(2)}) copy-start(f32[128,2048]{1,0:T(8,128)S(1)} %get-tuple-element.1042) | copy-start | bytes 3145732
  285.7 744.5 %all-gather.28.cloned.1.call-start = ((), (), s32[]{:S(2)}) async-start(), calls=%async_computation.24 | async-start | bytes 4718592 | tf_op jit(solution)/shard_map/all_gather | solution.py:313
  301.5 368.7 %copy-start.8 = (bf16[128,2048]{1,0:T(8,128)(2,1)}, bf16[128,2048]{1,0:T(8,128)(2,1)S(1)}, u32[]{:S(2)}) copy-start(bf16[128,2048]{1,0:T(8,128)(2,1)S(1)} %multiply_convert_fusion.3) | copy-start | bytes 1572868
  470.6 411.8 %copy-start.14 = (bf16[1,128,2048]{2,1,0:T(8,128)(2,1)S(1)}, bf16[1,128,2048]{2,1,0:T(8,128)(2,1)}, u32[]{:S(2)}) copy-start(bf16[1,128,2048]{2,1,0:T(8,128)(2,1)} %param.22) | copy-start | bytes 1572868
  897.5 12.3 copy-start.10
  909.8 13.8 copy-start.15
  925.2 6.7 copy-start.6
  932.0 2.5 copy-start.1
  932.2 1.6 copy-start.3
  933.9 264.5 %reduce-scatter.49.cloned.1.call-start = ((), (), s32[]{:S(2)}) async-start(), calls=%async_computation.39 | async-start | bytes 1179648
  1005.9 16.8 copy-start.19
  1005.9 16.8 copy-start.21
  1038.9 1.4 copy-start.31
  1040.3 1.3 copy-start.30
  1049.0 1.4 copy-start.31
  1050.4 1.3 copy-start.30
  1059.0 1.4 copy-start.31
  1060.4 1.3 copy-start.30
  1069.1 1.4 copy-start.31
  1079.1 1.4 copy-start.31
  1080.5 1.3 copy-start.30
  1089.2 1.4 copy-start.31
  1090.6 1.3 copy-start.30
  1099.3 1.4 copy-start.31
  1100.7 1.3 copy-start.30
  1109.4 1.4 copy-start.31
  1110.8 2.2 copy-start.17
  1110.8 2.2 copy-start.26
  1113.0 1.6 copy-start.24
  1116.0 83.0 %reduce-scatter.25.cloned.1.call-start = ((), (), s32[]{:S(2)}) async-start(), calls=%async_computation.27 | async-start | bytes 2359296 | tf_op jit(solution)/shard_map/reduce_scatter | solution.py:113
  1117.9 104.3 %reduce-scatter.29.cloned.1.call-start = ((), (), s32[]{:S(2)}) async-start(), calls=%async_computation.29 | async-start | bytes 2359296 | tf_op jit(solution)/shard_map/reduce_scatter | solution.py:113
  1119.9 271.5 %reduce-scatter.21.cloned.1.call-start = ((), (), s32[]{:S(2)}) async-start(), calls=%async_computation.25 | async-start | bytes 18874368 | tf_op jit(solution)/shard_map/reduce_scatter | solution.py:113
  1128.2 1.4 copy-start.12
  1128.2 432.0 %reduce-scatter.33.cloned.1.call-start = ((), (), s32[]{:S(2)}) async-start(), calls=%async_computation.31 | async-start | bytes 18874368 | tf_op jit(solution)/shard_map/reduce_scatter | solution.py:113
  1137.8 866.8 %reduce-scatter.37.cloned.1.call-start = ((), (), s32[]{:S(2)}) async-start(), calls=%async_computation.33 | async-start | bytes 51904512 | tf_op jit(solution)/shard_map/reduce_scatter | solution.py:113
  1158.2 1290.8 %reduce-scatter.41.cloned.1.call-start = ((), (), s32[]{:S(2)}) async-start(), calls=%async_computation.35 | async-start | bytes 51904512 | tf_op jit(solution)/shard_map/reduce_scatter | solution.py:113
  1177.8 1715.5 %reduce-scatter.45.cloned.1.call-start = ((), (), s32[]{:S(2)}) async-start(), calls=%async_computation.37 | async-start | bytes 51904512 | tf_op jit(solution)/shard_map/reduce_scatter | solution.py:113
  1198.3 1720.3 %reduce-scatter.51.cloned.1.call-start = ((), (), s32[]{:S(2)}) async-start(), calls=%async_computation.40 | async-start | bytes 163840
  1198.9 1747.4 %reduce-scatter.27.cloned.1.call-start = ((), (), s32[]{:S(2)}) async-start(), calls=%async_computation.28 | async-start | bytes 327680 | tf_op jit(solution)/shard_map/reduce_scatter | solution.py:355
  1199.6 1774.2 %reduce-scatter.31.cloned.1.call-start = ((), (), s32[]{:S(2)}) async-start(), calls=%async_computation.30 | async-start | bytes 327680 | tf_op jit(solution)/shard_map/reduce_scatter | solution.py:356
  1222.3 1790.3 %reduce-scatter.23.cloned.1.call-start = ((), (), s32[]{:S(2)}) async-start(), calls=%async_computation.26 | async-start | bytes 2621440 | tf_op jit(solution)/shard_map/reduce_scatter | solution.py:354
  1391.4 1660.0 %reduce-scatter.35.cloned.1.call-start = ((), (), s32[]{:S(2)}) async-start(), calls=%async_computation.32 | async-start | bytes 2621440 | tf_op jit(solution)/shard_map/reduce_scatter | solution.py:357
  1560.2 1560.4 %reduce-scatter.39.cloned.1.call-start = ((), (), s32[]{:S(2)}) async-start(), calls=%async_computation.34 | async-start | bytes 7208960 | tf_op jit(solution)/shard_map/reduce_scatter | solution.py:358
  2004.6 1185.1 %reduce-scatter.43.cloned.1.call-start = ((), (), s32[]{:S(2)}) async-start(), calls=%async_computation.36 | async-start | bytes 7208960 | tf_op jit(solution)/shard_map/reduce_scatter | solution.py:359
  2449.0 810.0 %reduce-scatter.47.cloned.1.call-start = ((), (), s32[]{:S(2)}) async-start(), calls=%async_computation.38 | async-start | bytes 7208960 | tf_op jit(solution)/shard_map/reduce_scatter | solution.py:360
  2894.6 12.1 copy-start.13
  (7 other events, 8.0 us)
Sparse Core Ops, SparseCore 0:
  9.8 29.2 all-gather.11
  40.9 26.4 all-gather.13
  69.3 87.4 all-gather.15
  158.5 87.4 all-gather.17
  247.7 210.3 all-gather.19
  459.8 210.3 all-gather.21
  672.0 210.3 all-gather.23
  884.6 47.8 all-gather.25
  934.6 47.4 all-gather.27
  1116.1 32.6 reduce-scatter.48
  1151.1 34.2 reduce-scatter.24
  1187.5 34.6 reduce-scatter.28
  1224.6 166.7 reduce-scatter.20
  1393.6 166.6 reduce-scatter.32
  1562.4 442.1 reduce-scatter.36
  2006.8 442.1 reduce-scatter.40
  2451.2 442.1 reduce-scatter.44
  2895.9 22.6 reduce-scatter.50
  2921.9 24.3 reduce-scatter.26
  2949.5 24.3 reduce-scatter.30
  2977.4 35.1 reduce-scatter.22
  3016.1 35.1 reduce-scatter.34
  3054.9 65.6 reduce-scatter.38
  3124.0 65.6 reduce-scatter.42
  3193.3 65.6 reduce-scatter.46
where the time goes:
time: 3280 us; the launch traced here: 3270 us
  waiting for transfers between devices  2690 us (82%)
  matrix products  307 us (9%)
  other arithmetic  90.5 us (3%)
  blocking collectives  78.1 us (2%)
  local copies, waits for them, and re-layouts  58.3 us (2%)
    reduce_scatter x7, waiting for transfers between devices, reduce_pack(): lax.psum_scatter(weight_term(left, right), 'ctx', scatter_dimension=0, ti...  1690 us
    all_gather x1, waiting for transfers between devices, on_device(): lax.all_gather(w_down, 'fsdp', axis=0, tiled=True)  200 us
    all_gather x1, waiting for transfers between devices, on_device(): lax.all_gather(w_up, 'fsdp', axis=0, tiled=True)  200 us
    all_gather x1, waiting for transfers between devices, on_device(): lax.all_gather(w_gate, 'fsdp', axis=0, tiled=True)  157 us
    dot_general x7, matrix products, weight_term(): lax.dot_general(left, right, (((0,), (0,)), ((), ())), preferred_element_...  78.6 us
    reduce_scatter x1, waiting for transfers between devices, on_device(): lax.psum_scatter(pack_sums[4], 'fsdp', scatter_dimension=0, tiled=True)  69.3 us
    reduce_scatter x1, waiting for transfers between devices, on_device(): lax.psum_scatter(pack_sums[6], 'fsdp', scatter_dimension=0, tiled=True)  69.3 us
    reduce_scatter x1, waiting for transfers between devices, on_device(): lax.psum_scatter(pack_sums[5], 'fsdp', scatter_dimension=0, tiled=True)  69.1 us
  transfers between devices with their start and end apart: 25, of which 20 were waited for; matrix products, arithmetic and copies ran while one was open for 11% of the time, Pallas kernels for 0%

commit v1 on v0

v1 whole, which is shorter than its diff:
```python
import math

import jax
import jax.numpy as jnp
from jax import lax
from jax.sharding import PartitionSpec as P

HEADS = 32
KV_HEADS = 4
HEAD = 64
EPS = 1e-05
THETA = 10000.0
NEGATIVE = -1e30
BF = jnp.bfloat16
F32 = jnp.float32


def dot(left, right, dims, out=F32):
    return lax.dot_general(left, right, (dims, ((), ())), preferred_element_type=out)


def mm(left, right, out=F32):
    return dot(left, right, ((1,), (0,)), out)


def mm_nt(left, right, out=F32):
    return dot(left, right, ((1,), (1,)), out)


def mm_tn(left, right, out=F32):
    return dot(left, right, ((0,), (0,)), out)


def make_body(n_ctx, n_fsdp):
    nz = n_ctx // 2
    core_swap = [(i, i ^ 1) for i in range(n_ctx)]

    def shift(step):
        return [(i, ((i // 2 + step) % nz) * 2 + i % 2) for i in range(n_ctx)]

    def swap(x):
        return lax.ppermute(x, "ctx", core_swap)

    def gather_ctx(x):
        parts = [x] + [lax.ppermute(x, "ctx", shift(k)) for k in range(1, nz)]
        mine = jnp.concatenate(parts, 0)
        return jnp.concatenate([mine, swap(mine)], 0)

    def reduce_ctx(partial):
        rows = partial.shape[0] // (2 * nz)
        half = nz * rows
        other = swap(partial[half:])
        pair = partial[:half].astype(F32) + other.astype(F32)
        total = pair[:rows]
        low = pair.astype(BF)
        for k in range(1, nz):
            total = total + lax.ppermute(
                low[k * rows : (k + 1) * rows], "ctx", shift(nz - k)
            ).astype(F32)
        return total

    def body(
        tokens,
        cotangent,
        lengths,
        span_order,
        gain_attn,
        w_query,
        w_key,
        w_value,
        w_out,
        gain_ffn,
        w_gate,
        w_up,
        w_down,
    ):
        c = lax.axis_index("ctx")
        f = lax.axis_index("fsdp")
        z = c // 2
        p = c % 2
        tok = tokens.shape[1]
        span = tok // 2
        width = tokens.shape[2]
        rows_all = n_ctx * tok
        q_cols = HEADS * HEAD // n_ctx
        heads = HEADS // n_ctx
        kv = c * KV_HEADS // n_ctx
        ff = w_gate.shape[1]
        ff_c = ff // n_ctx
        ff_b = ff_c // n_fsdp
        shard = w_query.shape[0]
        score_scale = 1.0 / math.sqrt(HEAD)

        row = jnp.arange(rows_all, dtype=jnp.int32)
        block = row // tok
        dealt_dev = ((z - block % nz) % nz) * 2 + (p ^ (block // nz))
        slot = dealt_dev * 2 + (row % tok) // span
        slot_table = jnp.arange(span_order.shape[1], dtype=jnp.int32)
        chosen = jnp.sum(
            jnp.where(slot[:, None] == slot_table[None, :], span_order[0][None, :], 0), axis=1
        )
        anchor = chosen * span + row % span
        ends = jnp.cumsum(lengths[0])
        starts = ends - lengths[0]
        segment = jnp.sum((anchor[:, None] >= ends[None, :]).astype(jnp.int32), axis=1)
        first = jnp.sum(
            jnp.where(
                segment[:, None] == jnp.arange(ends.shape[0], dtype=jnp.int32)[None, :],
                starts[None, :],
                0,
            ),
            axis=1,
        )
        pos = anchor - first
        half_dim = HEAD // 2
        inverse = THETA ** (-(jnp.arange(half_dim, dtype=F32) * 2.0 / HEAD))
        angles = pos.astype(F32)[:, None] * inverse[None, :]
        cosine = jnp.cos(angles)[:, None, :]
        sine = jnp.sin(angles)[:, None, :]
        allowed = (segment[:, None] == segment[None, :]) & (pos[None, :] <= pos[:, None])

        def rotate(v, sign):
            a, b = v[..., :half_dim], v[..., half_dim:]
            return jnp.concatenate(
                [a * cosine - sign * b * sine, b * cosine + sign * a * sine], axis=-1
            )

        g1 = gain_attn.astype(F32)[:, None]
        g2 = gain_ffn.astype(F32)[:, None]

        def cols(w, start, size):
            return lax.dynamic_slice_in_dim(w, start, size, 1)

        wq = cols(w_query, c * q_cols, q_cols)
        wk = cols(w_key, kv * HEAD, HEAD)
        wv = cols(w_value, kv * HEAD, HEAD)
        wqkv_loc = (jnp.concatenate([wq, wk, wv], 1).astype(F32) * g1).astype(BF)
        pad = wqkv_loc.shape[1]
        gains = jnp.concatenate([gain_attn, gain_ffn])
        extra = 16
        gains = jnp.pad(gains, (0, extra * pad - gains.shape[0])).reshape(extra, pad)
        small = lax.all_gather(jnp.concatenate([wqkv_loc, gains], 0), "fsdp", axis=0)
        wqkv = small[:, :shard].reshape(width, pad)
        gains_all = small[:, shard:].reshape(n_fsdp, extra * pad)[:, : 2 * shard]
        gain1 = gains_all[:, :shard].reshape(width).astype(F32)
        gain2 = gains_all[:, shard:].reshape(width).astype(F32)

        wo = lax.all_gather(w_out, "fsdp", axis=0, tiled=True)
        wg = lax.all_gather(
            (cols(w_gate, c * ff_c, ff_c).astype(F32) * g2).astype(BF), "fsdp", axis=0, tiled=True
        )
        wu = lax.all_gather(
            (cols(w_up, c * ff_c, ff_c).astype(F32) * g2).astype(BF), "fsdp", axis=0, tiled=True
        )
        per_shard = w_down.shape[0] // ff_c
        source = c // per_shard
        inner = (c % per_shard) * ff_c
        wd_block = jnp.where(
            f == source, lax.dynamic_slice_in_dim(w_down, inner + f * ff_b, ff_b, 0), 0
        )
        for k in range(1, n_fsdp):
            send = lax.dynamic_slice_in_dim(
                w_down, inner + ((f + k) % n_fsdp) * ff_b, ff_b, 0
            )
            pairs = [
                (
                    ci * n_fsdp + ci // per_shard,
                    ci * n_fsdp + (ci // per_shard + k) % n_fsdp,
                )
                for ci in range(n_ctx)
            ]
            wd_block = wd_block + lax.ppermute(send, ("ctx", "fsdp"), pairs)
        wd = lax.all_gather(wd_block, "fsdp", axis=0, tiled=True)

        x = gather_ctx(tokens[0])
        cot = gather_ctx(cotangent[0])
        xf = x.astype(F32)
        r1 = lax.rsqrt(jnp.mean(xf * xf, axis=-1, keepdims=True) + EPS)
        qkv = mm(x, wqkv) * r1
        q = rotate(qkv[:, :q_cols].reshape(rows_all, heads, HEAD), 1.0).astype(BF)
        k = rotate(qkv[:, q_cols : q_cols + HEAD].reshape(rows_all, 1, HEAD), 1.0).astype(BF)[:, 0]
        v = qkv[:, q_cols + HEAD :].astype(BF)
        scores = jnp.einsum("thd,ud->htu", q, k, preferred_element_type=F32)
        scores = jnp.where(allowed[None], scores * score_scale, NEGATIVE)
        top = jnp.max(scores, axis=-1, keepdims=True)
        log_norm = top + jnp.log(jnp.sum(jnp.exp(scores - top), axis=-1, keepdims=True))
        probs = jnp.exp(scores - log_norm)
        weights = probs.astype(BF)
        att = jnp.einsum("htu,ud->thd", weights, v, preferred_element_type=F32)
        attended = att.astype(BF).reshape(rows_all, q_cols)

        same = jnp.concatenate(
            [attended], 0
        )
        def blocks(v2, b):
            return v2[b * tok : (b + 1) * tok]

        got = []
        for qq in range(2):
            for kk in range(nz):
                piece = blocks(attended, qq * nz + kk)
                perm = [
                    (i, ((i // 2 - kk) % nz) * 2 + ((i % 2) ^ qq)) for i in range(n_ctx)
                ]
                got.append(piece if (qq == 0 and kk == 0) else lax.ppermute(piece, "ctx", perm))
        full = jnp.stack(got, 0)
        order = jnp.arange(n_ctx, dtype=jnp.int32)
        pick = ((order % 2) ^ p) * nz + (order // 2 - z) % nz
        own_att = jnp.take(full, pick, axis=0).transpose(1, 0, 2).reshape(tok, width)
        inputs = tokens[0].astype(F32)
        hidden = inputs + mm(own_att, wo)
        r2_own = lax.rsqrt(jnp.mean(hidden * hidden, axis=-1, keepdims=True) + EPS)
        h = gather_ctx(hidden.astype(BF))
        hf = h.astype(F32)
        r2 = lax.rsqrt(jnp.mean(hf * hf, axis=-1, keepdims=True) + EPS)
        gate = mm(h, wg) * r2
        up = mm(h, wu) * r2
        sig = jax.nn.sigmoid(gate)
        act = (gate * sig * up).astype(BF)
        act_grad = mm_nt(cot, wd) * r2
        gg = (act_grad * up * sig * (1.0 + gate * (1.0 - sig))).astype(BF)
        ug = (act_grad * gate * sig).astype(BF)
        n2 = reduce_ctx((mm_nt(gg, wg) + mm_nt(ug, wu)).astype(BF))
        hidden_grad = (
            cotangent[0].astype(F32)
            + n2
            - hidden * (r2_own * r2_own * jnp.mean(n2 * hidden, axis=-1, keepdims=True))
        )
        branch = hidden_grad.astype(BF)
        branch_all = gather_ctx(branch)
        wo_c = lax.dynamic_slice_in_dim(wo, c * q_cols, q_cols, 0)
        agrad = mm_nt(branch_all, wo_c).astype(BF)
        output = (hidden + reduce_ctx(mm(act, wd).astype(BF))).astype(BF)

        ag3 = agrad.reshape(rows_all, heads, HEAD)
        pgrad = jnp.einsum("thd,ud->htu", ag3, v, preferred_element_type=F32)
        delta = jnp.sum(probs * pgrad, axis=-1, keepdims=True)
        sgrad = (probs * (pgrad - delta)).astype(BF)
        dq = jnp.einsum("htu,ud->thd", sgrad, k, preferred_element_type=F32) * score_scale
        dk = jnp.einsum("htu,thd->ud", sgrad, q, preferred_element_type=F32) * score_scale
        dv = jnp.einsum("htu,thd->ud", weights, ag3, preferred_element_type=F32)
        dqkv = jnp.concatenate(
            [
                rotate(dq, -1.0).reshape(rows_all, q_cols),
                rotate(dk[:, None, :], -1.0)[:, 0],
                dv,
            ],
            1,
        )
        dqkv = (dqkv * r1).astype(BF)
        n1 = reduce_ctx(mm_nt(dqkv, wqkv).astype(BF))
        r1_own = r1[:tok]
        grad_in = (
            hidden_grad
            + n1
            - inputs * (r1_own * r1_own * jnp.mean(n1 * inputs, axis=-1, keepdims=True))
        ).astype(BF)

        e_down = mm_tn(act, cot, BF)
        e_out = mm_tn(attended, branch_all, BF)
        e_cols = jnp.concatenate([mm_tn(h, gg, BF), mm_tn(h, ug, BF), mm_tn(x, dqkv, BF)], 1)
        rows_b = width // (n_ctx * n_fsdp)
        gd = lax.psum_scatter(e_down, "fsdp", scatter_dimension=0, tiled=True)
        go = lax.psum_scatter(e_out, "fsdp", scatter_dimension=0, tiled=True)
        ec = e_cols.reshape(n_ctx, n_fsdp, rows_b, e_cols.shape[1]).transpose(1, 0, 2, 3)
        ec = ec.reshape(n_fsdp, n_ctx * rows_b, e_cols.shape[1])
        ec = lax.psum_scatter(ec, "fsdp", scatter_dimension=0, tiled=True)[0]
        w_cols = jnp.concatenate([wg, wu, wqkv], 1).reshape(n_ctx, n_fsdp, rows_b, -1)
        w_mine = lax.dynamic_index_in_dim(w_cols, f, 1, keepdims=False)
        prod = ec.reshape(n_ctx, rows_b, -1).astype(F32) * w_mine.astype(F32)
        s2 = jnp.sum(prod[..., : 2 * ff_c], axis=-1, keepdims=True)
        s1 = jnp.sum(prod[..., 2 * ff_c :], axis=-1, keepdims=True)
        tail = jnp.concatenate([s1, s2, jnp.zeros((n_ctx, rows_b, 126), F32)], -1).astype(BF)
        ship = jnp.concatenate([ec.reshape(n_ctx, rows_b, -1), tail], -1)
        recv = lax.all_to_all(ship, "ctx", 0, 0, tiled=True)
        my_row = (c * n_fsdp + f) * rows_b
        gain1_r = lax.dynamic_slice_in_dim(gain1, my_row, rows_b, 0)
        gain2_r = lax.dynamic_slice_in_dim(gain2, my_row, rows_b, 0)
        recv = recv.astype(F32)

        def lay(start, size):
            return recv[:, :, start : start + size].transpose(1, 0, 2).reshape(rows_b, -1)

        grad_gate = lay(0, ff_c) * gain2_r[:, None]
        grad_up = lay(ff_c, ff_c) * gain2_r[:, None]
        grad_query = lay(2 * ff_c, q_cols) * gain1_r[:, None]
        share = n_ctx // KV_HEADS

        def lay_kv(start):
            part = recv[:, :, start : start + HEAD].reshape(KV_HEADS, share, rows_b, HEAD)
            return jnp.sum(part, 1).transpose(1, 0, 2).reshape(rows_b, -1) * gain1_r[:, None]

        grad_key = lay_kv(2 * ff_c + q_cols)
        grad_value = lay_kv(2 * ff_c + q_cols + HEAD)
        sums = jnp.sum(recv[:, :, -128:-126], 0)
        grad_g1 = sums[:, 0] / gain1_r
        grad_g2 = sums[:, 1] / gain2_r
        return (
            output[None],
            grad_in[None],
            grad_g1,
            grad_query,
            grad_key,
            grad_value,
            go.astype(F32),
            grad_g2,
            grad_gate,
            grad_up,
            gd.astype(F32),
        )

    return body


def solution(mesh):
    body = make_body(mesh.shape["ctx"], mesh.shape["fsdp"])
    both = ("ctx", "fsdp")
    in_specs = (
        P("fsdp", "ctx", None),
        P("fsdp", "ctx", None),
        P("fsdp", None),
        P("fsdp", None),
        P("fsdp"),
        P("fsdp", None),
        P("fsdp", None),
        P("fsdp", None),
        P("fsdp", None),
        P("fsdp"),
        P("fsdp", None),
        P("fsdp", None),
        P("fsdp", None),
    )
    out_specs = (
        P("fsdp", "ctx", None),
        P("fsdp", "ctx", None),
        P(both),
        P(both, None),
        P(both, None),
        P(both, None),
        P(both, None),
        P(both),
        P(both, None),
        P(both, None),
        P(both, None),
    )
    return jax.shard_map(body, mesh=mesh, in_specs=in_specs, out_specs=out_specs, check_vma=False)
```

time: 3280 us -> 771 us (0.24)
  waiting for transfers between devices: 2690 us -> 375 us
  matrix products: 307 us -> 116 us
  starting transfers between devices: 1.7 us -> 90.4 us
  blocking collectives: 78.1 us -> 0 us
    reduce_scatter x14 -> x2, waiting for transfers between devices: 2030 us -> 43.9 us  [the longest x1 29.1 us: body(): go = lax.psum_scatter(e_out, 'fsdp', scatter_dimension=0, tiled=True)]
    all_gather x9 -> x5, waiting for transfers between devices: 645 us -> 17.7 us  [the longest x1 17.7 us: body(): wd = lax.all_gather(wd_block, 'fsdp', axis=0, tiled=True)]
    ppermute x0 -> x38, waiting for transfers between devices: none -> 261 us  [the longest x12 118 us: gather_ctx(): parts = [x] + [lax.ppermute(x, 'ctx', shift(k)) for k in range(1, nz)]]
    dot_general x77 -> x21, matrix products: 307 us -> 116 us  [the longest x15 83.6 us: dot(): lax.dot_general(left, right, (dims, ((), ())), preferred_element_type=out)]
    ppermute x0 -> x38, starting transfers between devices: none -> 85.3 us  [the longest x12 60.7 us: gather_ctx(): parts = [x] + [lax.ppermute(x, 'ctx', shift(k)) for k in range(1, nz)]]
    all_gather x6 -> x0, blocking collectives: 78.1 us -> none  [the longest x1 15.6 us: on_device(): lax.all_gather(log_norm_rows, 'ctx', axis=0, tiled=True)]
    reduce_sum x109 -> x12, other arithmetic: 76.2 us -> 17 us  [the longest x1 7.98 us: body(): jnp.sum(jnp.exp(scores - top), axis=-1, keepdims=True)]
    unnamed x27 -> x9, waiting for transfers between devices: 16.6 us -> 52.3 us
  transfers between devices with their start and end apart: 25 -> 47, of which waited for: 20 -> 23; matrix products, arithmetic and copies ran while one was open for 11% -> 22% of each run, Pallas kernels for 0% -> 0%
where the time goes in v1:
time: 771 us; the launch traced here: 765 us
  waiting for transfers between devices  375 us (49%)
  matrix products  116 us (15%)
  starting transfers between devices  90.4 us (12%)
  local copies, waits for them, and re-layouts  88.1 us (11%)
  other arithmetic  80 us (10%)
  between operations  15.9 us (2%)
    ppermute x12, waiting for transfers between devices, gather_ctx(): parts = [x] + [lax.ppermute(x, 'ctx', shift(k)) for k in range(1, nz)]  118 us
    ppermute x9, waiting for transfers between devices, reduce_ctx(): lax.ppermute(low[k * rows:(k + 1) * rows], 'ctx', shift(nz - k)).astype(F32)  109 us
    dot_general x15, matrix products, dot(): lax.dot_general(left, right, (dims, ((), ())), preferred_element_type=out)  83.6 us
    ppermute x12, starting transfers between devices, gather_ctx(): parts = [x] + [lax.ppermute(x, 'ctx', shift(k)) for k in range(1, nz)]  60.7 us
    unnamed x9, waiting for transfers between devices  52.3 us
    ppermute x7, waiting for transfers between devices, body(): lax.ppermute(piece, 'ctx', perm)  32.8 us
    reduce_scatter x1, waiting for transfers between devices, body(): go = lax.psum_scatter(e_out, 'fsdp', scatter_dimension=0, tiled=True)  29.1 us
    unnamed x146, local copies, waits for them, and re-layouts  23 us
  transfers between devices with their start and end apart: 47, of which 23 were waited for; matrix products, arithmetic and copies ran while one was open for 22% of the time, Pallas kernels for 0%

profile of v1, /device:TPU:0, one launch (start us, length us, event | category | flops | bytes accessed | tf_op | source)
XLA Modules:
  0.0 764.7 jit_solution(8235124281903732848)
XLA Ops:
  11.9 3.6 multiply_convert_fusion.4
  15.6 5.1 collective-permute-start.24
  27.0 3.0 constant_dynamic-slice_fusion.2
  30.0 25.6 %collective-permute-done.2 = bf16[128,2048]{1,0:T(8,128)(2,1)S(1)} collective-permute-done((bf16[128,2048]{1,0:T(8,128)(2,1)S(1)}, bf16[128,2048]{1,0:T(8,128)(2,1)S(1)}, u32[]{:S(2)}, u32[]{:S(2)}) %collective-permute-start.2) | collective-permute-done | bytes 524320 | tf_op jit(solution)/shard_map/ppermute | solution.py:45
  55.6 45.4 %collective-permute-start.22 = (bf16[128,2048]{1,0:T(8,128)(2,1)S(1)}, bf16[128,2048]{1,0:T(8,128)(2,1)S(1)}, u32[]{:S(2)}, u32[]{:S(2)}) collective-permute-start(bf16[128,2048]{1,0:T(8,128)(2,1)S(1)} %bitcast.189), channel_id=1, source_target_pairs={{0,8},{4,12},{8,16},{12,20},{16,24},{20,28},{24,0},{28,4},{1,9},{5... | collective-permute-start | bytes 1572872 | tf_op jit(solution)/shard_map/ppermute | solution.py:45
  100.9 9.6 %collective-permute-done.1 = bf16[128,2048]{1,0:T(8,128)(2,1)} collective-permute-done((bf16[128,2048]{1,0:T(8,128)(2,1)S(1)}, bf16[128,2048]{1,0:T(8,128)(2,1)}, u32[]{:S(2)}, u32[]{:S(2)}) %collective-permute-start.1) | collective-permute-done | bytes 524320 | tf_op jit(solution)/shard_map/ppermute | solution.py:45
  110.6 4.3 collective-permute-start.15
  114.8 2.7 pad_maximum_fusion.1
  135.0 3.8 constant_dynamic-update-slice_fusion
  138.8 3.1 multiply_reduce_fusion.1
  141.9 4.1 convolution_multiply_fusion
  147.9 7.3 fusion.114
  155.2 8.0 %exponential_reduce_fusion = f32[4,1024]{1,0:T(4,128)S(1)} fusion(f32[4,1024,1024]{1,2,0:T(8,128)} %get-tuple-element.80, f32[4,1024]{1,0:T(4,128)S(1)} %get-tuple-element.79), kind=kLoop, calls=%fused_computation.8 | loop fusion | flops 8384512 | bytes 16809984 | tf_op jit(solution)/shard_map/reduce_sum | solution.py:186
  163.3 8.4 %fusion.10 = bf16[64,4,1024]{2,0,1:T(8,128)(2,1)S(1)} fusion(f32[4,1024,1024]{1,2,0:T(8,128)} %get-tuple-element.80, f32[4,1024]{1,0:T(4,128)S(1)} %log_add_fusion, f32[1024,384]{0,1:T(8,128)S(1)} %convolution_multiply_fusion), kind=kOutput, calls=%fused_computation.44 | convolution fusion | flops 545521664 | bytes 17448960 | tf_op jit(solution)/shard_map/htu,ud->thd/dot_general | solution.py:189
  171.9 4.3 collective-permute-done.4
  176.2 5.4 collective-permute-done.5
  181.6 6.0 collective-permute-done.6
  189.0 4.0 collective-permute-done.8
  193.0 6.0 collective-permute-done.9
  199.0 5.9 collective-permute-done.10
  205.8 5.5 constant_dynamic-update-slice_fusion.10
  213.4 3.1 add_add_fusion
  216.8 9.1 %collective-permute-done.13 = bf16[128,2048]{1,0:T(8,128)(2,1)} collective-permute-done((bf16[128,2048]{1,0:T(8,128)(2,1)S(1)}, bf16[128,2048]{1,0:T(8,128)(2,1)}, u32[]{:S(2)}, u32[]{:S(2)}) %collective-permute-start.13) | collective-permute-done | bytes 524320 | tf_op jit(solution)/shard_map/ppermute | solution.py:45
  225.9 31.2 %collective-permute-done.12 = bf16[128,2048]{1,0:T(8,128)(2,1)} collective-permute-done((bf16[128,2048]{1,0:T(8,128)(2,1)S(1)}, bf16[128,2048]{1,0:T(8,128)(2,1)}, u32[]{:S(2)}, u32[]{:S(2)}) %collective-permute-start.12) | collective-permute-done | bytes 524320 | tf_op jit(solution)/shard_map/ppermute | solution.py:45
  268.1 8.1 %fusion.116 = f32[1024,704]{0,1:T(8,128)} fusion(bf16[1024,2048]{1,0:T(8,128)(2,1)} %copy-done.9, bf16[2048,704]{1,0:T(8,128)(2,1)} %all-gather.11.cloned.1.call-done), kind=kOutput, calls=%fused_computation.268 | convolution fusion | flops 2952790016 | bytes 9961472 | tf_op jit(solution)/shard_map/dot_general | solution.py:19
  276.2 7.9 %fusion.115 = f32[1024,704]{0,1:T(8,128)} fusion(bf16[1024,2048]{1,0:T(8,128)(2,1)} %copy-done.9, bf16[2048,704]{1,0:T(8,128)(2,1)} %all-gather.9.cloned.1.call-done), kind=kOutput, calls=%fused_computation.267 | convolution fusion | flops 2952790016 | bytes 9961472 | tf_op jit(solution)/shard_map/dot_general | solution.py:19
  284.2 17.7 %all-gather.13.cloned.1.call-done = bf16[704,2048]{1,0:T(8,128)(2,1)} async-done(((bf16[176,2048]{1,0:T(8,128)(2,1)}), bf16[704,2048]{1,0:T(8,128)(2,1)}) %all-gather.13.cloned.1.call-update) | async-done | bytes 2883600 | tf_op jit(solution)/shard_map/all_gather | solution.py:173
  301.9 10.4 %multiply_convert_fusion = (bf16[1024,704]{0,1:T(8,128)(2,1)}, bf16[1024,704]{0,1:T(8,128)(2,1)S(1)}, bf16[1024,704]{0,1:T(8,128)(2,1)S(1)}) fusion(f32[1024,704]{0,1:T(8,128)} %fusion.115, f32[1024]{0:T(1024)S(1)} %add_rsqrt_fusion, f32[1024,704]{0,1:T(8,128)} %fusion.116, bf16[1024,2048]{1,0:T(8,128)(2,1)} %copy-done.42, ...), kind=kOutput, calls=%fused_computation.22 | convolution fusion | flops 2966487040 | bytes 17174528 | tf_op jit(solution)/shard_map/dot_general | solution.py:19
  313.3 4.1 convolution_convert_fusion.1
  319.3 5.8 fusion.117
  325.2 6.4 add_convert_fusion
  333.2 3.4 collective-permute-start.19
  338.9 2.8 collective-permute-start.27
  342.3 6.6 collective-permute-done.19
  350.4 10.8 %collective-permute-done.21 = bf16[128,2048]{1,0:T(8,128)(2,1)S(1)} collective-permute-done((bf16[128,2048]{1,0:T(8,128)(2,1)S(1)}, bf16[128,2048]{1,0:T(8,128)(2,1)S(1)}, u32[]{:S(2)}, u32[]{:S(2)}) %collective-permute-start.21) | collective-permute-done | bytes 524320 | tf_op jit(solution)/shard_map/ppermute | solution.py:57
  361.2 21.4 %collective-permute-done.20 = bf16[128,2048]{1,0:T(8,128)(2,1)S(1)} collective-permute-done((bf16[128,2048]{1,0:T(8,128)(2,1)S(1)}, bf16[128,2048]{1,0:T(8,128)(2,1)S(1)}, u32[]{:S(2)}, u32[]{:S(2)}) %collective-permute-start.20) | collective-permute-done | bytes 524320 | tf_op jit(solution)/shard_map/ppermute | solution.py:57
  382.7 12.3 %collective-permute-done.29 = bf16[128,2048]{1,0:T(8,128)(2,1)S(1)} collective-permute-done((bf16[128,2048]{1,0:T(8,128)(2,1)S(1)}, bf16[128,2048]{1,0:T(8,128)(2,1)S(1)}, u32[]{:S(2)}, u32[]{:S(2)}) %collective-permute-start.29) | collective-permute-done | bytes 524320 | tf_op jit(solution)/shard_map/ppermute | solution.py:57
  395.0 32.2 %collective-permute-done.28 = bf16[128,2048]{1,0:T(8,128)(2,1)S(1)} collective-permute-done((bf16[128,2048]{1,0:T(8,128)(2,1)S(1)}, bf16[128,2048]{1,0:T(8,128)(2,1)S(1)}, u32[]{:S(2)}, u32[]{:S(2)}) %collective-permute-start.28) | collective-permute-done | bytes 524320 | tf_op jit(solution)/shard_map/ppermute | solution.py:57
  433.6 11.8 %collective-permute-done.32 = bf16[128,2048]{1,0:T(8,128)(2,1)S(1)} collective-permute-done((bf16[128,2048]{1,0:T(8,128)(2,1)S(1)}, bf16[128,2048]{1,0:T(8,128)(2,1)S(1)}, u32[]{:S(2)}, u32[]{:S(2)}) %collective-permute-start.32) | collective-permute-done | bytes 524320 | tf_op jit(solution)/shard_map/ppermute | solution.py:45
  445.4 31.1 %collective-permute-done.31 = bf16[128,2048]{1,0:T(8,128)(2,1)S(1)} collective-permute-done((bf16[128,2048]{1,0:T(8,128)(2,1)S(1)}, bf16[128,2048]{1,0:T(8,128)(2,1)S(1)}, u32[]{:S(2)}, u32[]{:S(2)}) %collective-permute-start.31) | collective-permute-done | bytes 524320 | tf_op jit(solution)/shard_map/ppermute | solution.py:45
  476.9 3.6 fusion.121
  480.5 4.6 fusion.120
  489.3 4.1 convolution_convert_fusion.2
  493.5 3.4 fusion.15
  496.9 8.5 %fusion = (f32[4,1024]{1,0:T(4,128)S(1)}, f32[1024,1024,4]{1,0,2:T(8,128)}) fusion(f32[4,1024,1024]{1,2,0:T(8,128)S(1)} %bitcast.175, f32[4,1024]{1,0:T(4,128)S(1)} %log_add_fusion, bf16[1024,4,64]{0,2,1:T(8,128)(2,1)S(1)} %bitcast.194, f32[1024,384]{0,1:T(8,128)} %copy-done.17), kind=kOutput, calls=%fused_computation.3 | convolution fusion | flops 549449728 | bytes 34242560 | tf_op jit(solution)/shard_map/thd,ud->htu/dot_general | solution.py:236
  505.4 8.0 %fusion.2 = bf16[4,1024,1024]{1,2,0:T(8,128)(2,1)S(1)} fusion(f32[1024,1024,4]{1,0,2:T(8,128)} %get-tuple-element.83, f32[4,1024,1024]{1,2,0:T(8,128)S(1)} %bitcast.175, f32[4,1024]{1,0:T(4,128)S(1)} %get-tuple-element.82, f32[4,1024]{1,0:T(4,128)S(1)} %log_add_fusion), kind=kLoop, calls=%fused_computation.5 | loop fusion | flops 16777216 | bytes 41975808 | tf_op jit(solution)/shard_map/convert_element_type | solution.py:238
  513.5 2.7 fusion.14
  518.8 4.4 fusion.100
  523.2 3.7 pad_maximum_fusion
  527.0 10.1 %copy.87 = bf16[2048,1792]{1,0:T(8,128)(2,1)} copy(bf16[2048,1792]{0,1:T(8,128)(2,1)} %pad_maximum_fusion) | data formatting | bytes 14680064 | tf_op jit(solution)/shard_map/concatenate | solution.py:261
  537.0 6.9 copy.88
  544.0 7.8 %fusion.119 = bf16[704,2048]{1,0:T(8,128)(2,1)} fusion(bf16[1024,704]{0,1:T(8,128)(2,1)} %copy-done.54, bf16[1024,2048]{1,0:T(8,128)(2,1)} %copy-done.42), kind=kOutput, calls=%fused_computation.271 | convolution fusion | flops 2952790016 | bytes 8519680 | tf_op jit(solution)/shard_map/dot_general | solution.py:19
  558.3 13.2 %concatenate.104 = bf16[8,4,64,1792]{3,2,1,0:T(8,128)(2,1)} concatenate(bf16[8,4,64,704]{3,2,1,0:T(8,128)(2,1)} %bitcast.196, bf16[8,4,64,704]{3,2,1,0:T(8,128)(2,1)} %bitcast.195, bf16[8,4,64,384]{3,2,1,0:T(8,128)(2,1)S(1)} %bitcast.186), dimensions={3} | concatenate | bytes 14680064 | tf_op jit(solution)/shard_map/concatenate | solution.py:268
  571.5 51.5 %reduce-scatter.10.cloned.1.call-done = bf16[1,512,1792]{2,1,0:T(8,128)(2,1)} async-done(((bf16[4,512,1792]{2,1,0:T(8,128)(2,1)}), bf16[1,512,1792]{2,1,0:T(8,128)(2,1)}) %reduce-scatter.10.cloned.1.call-update) | async-done | bytes 1835024
  631.4 4.6 all-to-all-start
  636.1 4.4 fusion.118
  640.5 5.4 convert_add_fusion
  647.1 3.9 collective-permute-start.35
  653.0 14.8 %reduce-scatter.8.cloned.1.call-done = bf16[176,2048]{1,0:T(8,128)(2,1)} async-done(((bf16[704,2048]{1,0:T(8,128)(2,1)}), bf16[176,2048]{1,0:T(8,128)(2,1)}) %reduce-scatter.8.cloned.1.call-update) | async-done | bytes 720912 | tf_op jit(solution)/shard_map/reduce_scatter | solution.py:263
  670.2 29.1 %reduce-scatter.6.cloned.1.call-done = bf16[64,2048]{1,0:T(8,128)(2,1)} async-done(((bf16[256,2048]{1,0:T(8,128)(2,1)}), bf16[64,2048]{1,0:T(8,128)(2,1)}) %reduce-scatter.6.cloned.1.call-update) | async-done | bytes 262160 | tf_op jit(solution)/shard_map/reduce_scatter | solution.py:264
  701.1 26.1 %collective-permute-done.36 = bf16[128,2048]{1,0:T(8,128)(2,1)S(1)} collective-permute-done((bf16[128,2048]{1,0:T(8,128)(2,1)}, bf16[128,2048]{1,0:T(8,128)(2,1)S(1)}, u32[]{:S(2)}, u32[]{:S(2)}) %collective-permute-start.36) | collective-permute-done | bytes 524320 | tf_op jit(solution)/shard_map/ppermute | solution.py:57
  741.8 3.5 copy.97
  745.3 2.9 reshape.593
  754.2 3.3 broadcast_multiply_fusion
  (307 shorter events, 110.9 us)
Async XLA Ops:
  7.2 126.2 %all-gather.15.cloned.1.call-start = ((), (), s32[]{:S(2)}) async-start(), calls=%async_computation.10 | async-start | bytes 2027520 | tf_op jit(solution)/shard_map/all_gather | solution.py:142
  10.2 15.6 %copy-start.51 = (s32[1,4]{1,0:T(1,128)S(1)}, s32[1,4]{1,0:T(1,128)}, u32[]{:S(2)}) copy-start(s32[1,4]{1,0:T(1,128)} %param.15) | copy-start | bytes 52
  10.2 16.4 %copy-start.49 = (s32[1,16]{1,0:T(1,128)S(1)}, s32[1,16]{1,0:T(1,128)}, u32[]{:S(2)}) copy-start(s32[1,16]{1,0:T(1,128)} %param.16) | copy-start | bytes 196
  11.1 194.8 %all-gather.7.cloned.1.call-start = ((), (), s32[]{:S(2)}) async-start(), calls=%async_computation.4 | async-start | bytes 10485760 | tf_op jit(solution)/shard_map/all_gather | solution.py:148
  11.8 256.3 %all-gather.11.cloned.1.call-start = ((), (), s32[]{:S(2)}) async-start(), calls=%async_computation.6 | async-start | bytes 3932160 | tf_op jit(solution)/shard_map/all_gather | solution.py:152
  15.5 260.7 %all-gather.9.cloned.1.call-start = ((), (), s32[]{:S(2)}) async-start(), calls=%async_computation.5 | async-start | bytes 3932160 | tf_op jit(solution)/shard_map/all_gather | solution.py:149
  15.6 106.5 %collective-permute-start.24 = (bf16[128,2048]{1,0:T(8,128)(2,1)S(1)}, bf16[128,2048]{1,0:T(8,128)(2,1)S(1)}, u32[]{:S(2)}, u32[]{:S(2)}) collective-permute-start(bf16[128,2048]{1,0:T(8,128)(2,1)S(1)} %bitcast.187), channel_id=1, source_target_pairs={{0,24},{4,28},{8,0},{12,4},{16,8},{20,12},{24,16},{28,20},{1,25},{... | collective-permute-start | bytes 1572872 | tf_op jit(solution)/shard_map/ppermute | solution.py:45
  20.7 103.9 %collective-permute-start.23 = (bf16[128,2048]{1,0:T(8,128)(2,1)S(1)}, bf16[128,2048]{1,0:T(8,128)(2,1)S(1)}, u32[]{:S(2)}, u32[]{:S(2)}) collective-permute-start(bf16[128,2048]{1,0:T(8,128)(2,1)S(1)} %bitcast.188), channel_id=1, source_target_pairs={{0,16},{4,20},{8,24},{12,28},{16,0},{20,4},{24,8},{28,12},{1,17},{... | collective-permute-start | bytes 1572872 | tf_op jit(solution)/shard_map/ppermute | solution.py:45
  20.7 34.8 %collective-permute-start.2 = (bf16[128,2048]{1,0:T(8,128)(2,1)S(1)}, bf16[128,2048]{1,0:T(8,128)(2,1)S(1)}, u32[]{:S(2)}, u32[]{:S(2)}) collective-permute-start(bf16[128,2048]{1,0:T(8,128)(2,1)S(1)} %bitcast.178), channel_id=1, source_target_pairs={{0,24},{4,28},{8,0},{12,4},{16,8},{20,12},{24,16},{28,20},{1,25},{... | collective-permute-start | bytes 1572872 | tf_op jit(solution)/shard_map/ppermute | solution.py:45
  21.2 89.4 %collective-permute-start.1 = (bf16[128,2048]{1,0:T(8,128)(2,1)S(1)}, bf16[128,2048]{1,0:T(8,128)(2,1)}, u32[]{:S(2)}, u32[]{:S(2)}) collective-permute-start(bf16[128,2048]{1,0:T(8,128)(2,1)S(1)} %bitcast.179), channel_id=1, source_target_pairs={{0,16},{4,20},{8,24},{12,28},{16,0},{20,4},{24,8},{28,12},{1,17},{... | collective-permute-start | bytes 1572872 | tf_op jit(solution)/shard_map/ppermute | solution.py:45
  23.7 91.2 %collective-permute-start = (bf16[128,2048]{1,0:T(8,128)(2,1)S(1)}, bf16[128,2048]{1,0:T(8,128)(2,1)}, u32[]{:S(2)}, u32[]{:S(2)}) collective-permute-start(bf16[128,2048]{1,0:T(8,128)(2,1)S(1)} %bitcast.180), channel_id=1, source_target_pairs={{0,8},{4,12},{8,16},{12,20},{16,24},{20,28},{24,0},{28,4},{1,9},{5... | collective-permute-start | bytes 1572872 | tf_op jit(solution)/shard_map/ppermute | solution.py:45
  25.7 276.1 %all-gather.13.cloned.1.call-start = ((), (), s32[]{:S(2)}) async-start(), calls=%async_computation.7 | async-start | bytes 3604480 | tf_op jit(solution)/shard_map/all_gather | solution.py:173
  26.9 119.2 %copy-start.43 = (f32[32]{0:T(128)}, f32[32]{0:T(128)S(1)}, u32[]{:S(2)}) copy-start(f32[32]{0:T(128)S(1)} %negate_power_fusion) | copy-start | bytes 388
  27.0 119.1 %copy-start.40 = (f32[1024]{0:T(1024)}, f32[1024]{0:T(1024)S(1)}, u32[]{:S(2)}) copy-start(f32[1024]{0:T(1024)S(1)} %get-tuple-element.26) | copy-start | bytes 12292
  55.6 71.4 %collective-permute-start.22 = (bf16[128,2048]{1,0:T(8,128)(2,1)S(1)}, bf16[128,2048]{1,0:T(8,128)(2,1)S(1)}, u32[]{:S(2)}, u32[]{:S(2)}) collective-permute-start(bf16[128,2048]{1,0:T(8,128)(2,1)S(1)} %bitcast.189), channel_id=1, source_target_pairs={{0,8},{4,12},{8,16},{12,20},{16,24},{20,28},{24,0},{28,4},{1,9},{5... | collective-permute-start | bytes 1572872 | tf_op jit(solution)/shard_map/ppermute | solution.py:45
  110.6 100.8 %collective-permute-start.15 = (bf16[176,2048]{1,0:T(8,128)(2,1)}, bf16[176,2048]{1,0:T(8,128)(2,1)}, u32[]{:S(2)}, u32[]{:S(2)}) collective-permute-start(bf16[176,2048]{1,0:T(8,128)(2,1)} %get-tuple-element.37), channel_id=1, source_target_pairs={{0,1},{4,5},{9,10},{13,14},{18,19},{22,23},{27,24},{31,28}} | collective-permute-start | bytes 2162696 | tf_op jit(solution)/shard_map/ppermute | solution.py:172
  117.6 17.4 %collective-permute-start.3 = (bf16[512,2048]{1,0:T(8,128)(2,1)}, bf16[512,2048]{1,0:T(8,128)(2,1)}, u32[]{:S(2)}, u32[]{:S(2)}) collective-permute-start(bf16[512,2048]{1,0:T(8,128)(2,1)} %pad_maximum_fusion.1), channel_id=1, source_target_pairs={{0,4},{4,0},{8,12},{12,8},{16,20},{20,16},{24,28},{28,24},{1,5},{5... | collective-permute-start | bytes 6291464 | tf_op jit(solution)/shard_map/ppermute | solution.py:42
  122.1 89.2 %collective-permute-start.17 = (bf16[176,2048]{1,0:T(8,128)(2,1)}, bf16[176,2048]{1,0:T(8,128)(2,1)}, u32[]{:S(2)}, u32[]{:S(2)}) collective-permute-start(bf16[176,2048]{1,0:T(8,128)(2,1)} %get-tuple-element.38), channel_id=1, source_target_pairs={{0,3},{4,7},{9,8},{13,12},{18,17},{22,21},{27,26},{31,30}} | collective-permute-start | bytes 2162696 | tf_op jit(solution)/shard_map/ppermute | solution.py:172
  124.6 88.8 %collective-permute-start.16 = (bf16[176,2048]{1,0:T(8,128)(2,1)}, bf16[176,2048]{1,0:T(8,128)(2,1)}, u32[]{:S(2)}, u32[]{:S(2)}) collective-permute-start(bf16[176,2048]{1,0:T(8,128)(2,1)} %get-tuple-element.39), channel_id=1, source_target_pairs={{0,2},{4,6},{9,11},{13,15},{18,16},{22,20},{27,25},{31,29}} | collective-permute-start | bytes 2162696 | tf_op jit(solution)/shard_map/ppermute | solution.py:172
  128.6 130.4 %collective-permute-start.25 = (bf16[512,2048]{1,0:T(8,128)(2,1)}, bf16[512,2048]{1,0:T(8,128)(2,1)}, u32[]{:S(2)}, u32[]{:S(2)}) collective-permute-start(bf16[512,2048]{1,0:T(8,128)(2,1)} %pad_maximum_fusion.3), channel_id=1, source_target_pairs={{0,4},{4,0},{8,12},{12,8},{16,20},{20,16},{24,28},{28,24},{1,5},{5... | collective-permute-start | bytes 6291464 | tf_op jit(solution)/shard_map/ppermute | solution.py:42
  146.0 17.3 %copy-start.17 = (f32[1024,384]{0,1:T(8,128)}, f32[1024,384]{0,1:T(8,128)S(1)}, u32[]{:S(2)}) copy-start(f32[1024,384]{0,1:T(8,128)S(1)} %convolution_multiply_fusion) | copy-start | bytes 4718596
  163.2 42.4 %copy-start.48 = (pred[8]{0:T(512)(128)(4,1)S(1)}, pred[8]{0:T(512)(128)(4,1)}, u32[]{:S(2)}) copy-start(pred[8]{0:T(512)(128)(4,1)} %compare_and_fusion.1) | copy-start | bytes 28
  171.7 34.1 %copy-start.18 = (bf16[64,4,1024]{2,0,1:T(8,128)(2,1)}, bf16[64,4,1024]{2,0,1:T(8,128)(2,1)S(1)}, u32[]{:S(2)}) copy-start(bf16[64,4,1024]{2,0,1:T(8,128)(2,1)S(1)} %fusion.10) | copy-start | bytes 1572868
  171.9 4.3 collective-permute-start.4
  176.2 5.4 collective-permute-start.5
  181.6 6.1 collective-permute-start.6
  187.7 1.3 collective-permute-start.7
  189.0 4.1 collective-permute-start.8
  193.0 6.0 collective-permute-start.9
  199.0 5.9 collective-permute-start.10
  211.3 14.6 %collective-permute-start.13 = (bf16[128,2048]{1,0:T(8,128)(2,1)S(1)}, bf16[128,2048]{1,0:T(8,128)(2,1)}, u32[]{:S(2)}, u32[]{:S(2)}) collective-permute-start(bf16[128,2048]{1,0:T(8,128)(2,1)S(1)} %get-tuple-element.25), channel_id=1, source_target_pairs={{0,24},{4,28},{8,0},{12,4},{16,8},{20,12},{24,16},{28,20},{1,25},{... | collective-permute-start | bytes 1572872 | tf_op jit(solution)/shard_map/ppermute | solution.py:45
  211.3 45.8 %collective-permute-start.12 = (bf16[128,2048]{1,0:T(8,128)(2,1)S(1)}, bf16[128,2048]{1,0:T(8,128)(2,1)}, u32[]{:S(2)}, u32[]{:S(2)}) collective-permute-start(bf16[128,2048]{1,0:T(8,128)(2,1)S(1)} %get-tuple-element.25), channel_id=1, source_target_pairs={{0,16},{4,20},{8,24},{12,28},{16,0},{20,4},{24,8},{28,12},{1,17},{... | collective-permute-start | bytes 1572872 | tf_op jit(solution)/shard_map/ppermute | solution.py:45
  211.3 45.8 %collective-permute-start.11 = (bf16[128,2048]{1,0:T(8,128)(2,1)S(1)}, bf16[128,2048]{1,0:T(8,128)(2,1)}, u32[]{:S(2)}, u32[]{:S(2)}) collective-permute-start(bf16[128,2048]{1,0:T(8,128)(2,1)S(1)} %get-tuple-element.25), channel_id=1, source_target_pairs={{0,8},{4,12},{8,16},{12,20},{16,24},{20,28},{24,0},{28,4},{1,9},{5... | collective-permute-start | bytes 1572872 | tf_op jit(solution)/shard_map/ppermute | solution.py:45
  216.5 42.3 %copy-start.23 = (bf16[128,2048]{1,0:T(8,128)(2,1)S(1)}, bf16[128,2048]{1,0:T(8,128)(2,1)}, u32[]{:S(2)}) copy-start(bf16[128,2048]{1,0:T(8,128)(2,1)} %copy-done.22) | copy-start | bytes 1572868
  216.5 42.4 %copy-start.21 = (bf16[128,2048]{1,0:T(8,128)(2,1)S(1)}, bf16[128,2048]{1,0:T(8,128)(2,1)}, u32[]{:S(2)}) copy-start(bf16[128,2048]{1,0:T(8,128)(2,1)} %copy-done.20) | copy-start | bytes 1572868
  216.6 406.5 %reduce-scatter.10.cloned.1.call-start = ((), (), s32[]{:S(2)}) async-start(), calls=%async_computation.11 | async-start | bytes 9175040
  216.8 42.0 %copy-start.25 = (bf16[128,2048]{1,0:T(8,128)(2,1)S(1)}, bf16[128,2048]{1,0:T(8,128)(2,1)}, u32[]{:S(2)}) copy-start(bf16[128,2048]{1,0:T(8,128)(2,1)} %copy-done.24) | copy-start | bytes 1572868
  258.6 6.4 collective-permute-start.14
  317.7 14.2 %collective-permute-start.18 = (bf16[512,2048]{1,0:T(8,128)(2,1)S(1)}, bf16[512,2048]{1,0:T(8,128)(2,1)S(1)}, u32[]{:S(2)}, u32[]{:S(2)}) collective-permute-start(bf16[512,2048]{1,0:T(8,128)(2,1)S(1)} %slice.261), channel_id=1, source_target_pairs={{0,4},{4,0},{8,12},{12,8},{16,20},{20,16},{24,28},{28,24},{1,5},{5... | collective-permute-start | bytes 6291464 | tf_op jit(solution)/shard_map/ppermute | solution.py:42
  331.8 5.8 collective-permute-start.26
  333.2 15.7 %collective-permute-start.19 = (bf16[128,2048]{1,0:T(8,128)(2,1)S(1)}, bf16[128,2048]{1,0:T(8,128)(2,1)S(1)}, u32[]{:S(2)}, u32[]{:S(2)}) collective-permute-start(bf16[128,2048]{1,0:T(8,128)(2,1)S(1)} %get-tuple-element.48), channel_id=1, source_target_pairs={{0,24},{4,28},{8,0},{12,4},{16,8},{20,12},{24,16},{28,20},{1,25},{... | collective-permute-start | bytes 1572872 | tf_op jit(solution)/shard_map/ppermute | solution.py:57
  336.5 24.7 %collective-permute-start.21 = (bf16[128,2048]{1,0:T(8,128)(2,1)S(1)}, bf16[128,2048]{1,0:T(8,128)(2,1)S(1)}, u32[]{:S(2)}, u32[]{:S(2)}) collective-permute-start(bf16[128,2048]{1,0:T(8,128)(2,1)S(1)} %get-tuple-element.49), channel_id=1, source_target_pairs={{0,8},{4,12},{8,16},{12,20},{16,24},{20,28},{24,0},{28,4},{1,9},{5... | collective-permute-start | bytes 1572872 | tf_op jit(solution)/shard_map/ppermute | solution.py:57
  336.6 46.1 %collective-permute-start.20 = (bf16[128,2048]{1,0:T(8,128)(2,1)S(1)}, bf16[128,2048]{1,0:T(8,128)(2,1)S(1)}, u32[]{:S(2)}, u32[]{:S(2)}) collective-permute-start(bf16[128,2048]{1,0:T(8,128)(2,1)S(1)} %get-tuple-element.50), channel_id=1, source_target_pairs={{0,16},{4,20},{8,24},{12,28},{16,0},{20,4},{24,8},{28,12},{1,17},{... | collective-permute-start | bytes 1572872 | tf_op jit(solution)/shard_map/ppermute | solution.py:57
  338.9 43.8 %collective-permute-start.27 = (bf16[128,2048]{1,0:T(8,128)(2,1)S(1)}, bf16[128,2048]{1,0:T(8,128)(2,1)S(1)}, u32[]{:S(2)}, u32[]{:S(2)}) collective-permute-start(bf16[128,2048]{1,0:T(8,128)(2,1)S(1)} %get-tuple-element.45), channel_id=1, source_target_pairs={{0,24},{4,28},{8,0},{12,4},{16,8},{20,12},{24,16},{28,20},{1,25},{... | collective-permute-start | bytes 1572872 | tf_op jit(solution)/shard_map/ppermute | solution.py:57
  341.7 53.3 %collective-permute-start.29 = (bf16[128,2048]{1,0:T(8,128)(2,1)S(1)}, bf16[128,2048]{1,0:T(8,128)(2,1)S(1)}, u32[]{:S(2)}, u32[]{:S(2)}) collective-permute-start(bf16[128,2048]{1,0:T(8,128)(2,1)S(1)} %get-tuple-element.46), channel_id=1, source_target_pairs={{0,8},{4,12},{8,16},{12,20},{16,24},{20,28},{24,0},{28,4},{1,9},{5... | collective-permute-start | bytes 1572872 | tf_op jit(solution)/shard_map/ppermute | solution.py:57
  348.9 78.2 %collective-permute-start.28 = (bf16[128,2048]{1,0:T(8,128)(2,1)S(1)}, bf16[128,2048]{1,0:T(8,128)(2,1)S(1)}, u32[]{:S(2)}, u32[]{:S(2)}) collective-permute-start(bf16[128,2048]{1,0:T(8,128)(2,1)S(1)} %get-tuple-element.47), channel_id=1, source_target_pairs={{0,16},{4,20},{8,24},{12,28},{16,0},{20,4},{24,8},{28,12},{1,17},{... | collective-permute-start | bytes 1572872 | tf_op jit(solution)/shard_map/ppermute | solution.py:57
  428.7 48.2 %copy-start.10 = (bf16[1024,2048]{1,0:T(8,128)(2,1)S(1)}, bf16[1024,2048]{1,0:T(8,128)(2,1)}, u32[]{:S(2)}) copy-start(bf16[1024,2048]{1,0:T(8,128)(2,1)} %copy-done.9) | copy-start | bytes 12582916
  428.7 48.2 %copy-start.55 = (bf16[1024,704]{0,1:T(8,128)(2,1)S(1)}, bf16[1024,704]{0,1:T(8,128)(2,1)}, u32[]{:S(2)}) copy-start(bf16[1024,704]{0,1:T(8,128)(2,1)} %get-tuple-element.34) | copy-start | bytes 4325380
  430.4 15.0 %collective-permute-start.32 = (bf16[128,2048]{1,0:T(8,128)(2,1)S(1)}, bf16[128,2048]{1,0:T(8,128)(2,1)S(1)}, u32[]{:S(2)}, u32[]{:S(2)}) collective-permute-start(bf16[128,2048]{1,0:T(8,128)(2,1)S(1)} %get-tuple-element.22), channel_id=1, source_target_pairs={{0,24},{4,28},{8,0},{12,4},{16,8},{20,12},{24,16},{28,20},{1,25},{... | collective-permute-start | bytes 1572872 | tf_op jit(solution)/shard_map/ppermute | solution.py:45
  433.0 43.5 %collective-permute-start.31 = (bf16[128,2048]{1,0:T(8,128)(2,1)S(1)}, bf16[128,2048]{1,0:T(8,128)(2,1)S(1)}, u32[]{:S(2)}, u32[]{:S(2)}) collective-permute-start(bf16[128,2048]{1,0:T(8,128)(2,1)S(1)} %get-tuple-element.22), channel_id=1, source_target_pairs={{0,16},{4,20},{8,24},{12,28},{16,0},{20,4},{24,8},{28,12},{1,17},{... | collective-permute-start | bytes 1572872 | tf_op jit(solution)/shard_map/ppermute | solution.py:45
  433.0 43.5 %collective-permute-start.30 = (bf16[128,2048]{1,0:T(8,128)(2,1)S(1)}, bf16[128,2048]{1,0:T(8,128)(2,1)S(1)}, u32[]{:S(2)}, u32[]{:S(2)}) collective-permute-start(bf16[128,2048]{1,0:T(8,128)(2,1)S(1)} %get-tuple-element.22), channel_id=1, source_target_pairs={{0,8},{4,12},{8,16},{12,20},{16,24},{20,28},{24,0},{28,4},{1,9},{5... | collective-permute-start | bytes 1572872 | tf_op jit(solution)/shard_map/ppermute | solution.py:45
  476.8 10.9 %collective-permute-start.33 = (bf16[512,2048]{1,0:T(8,128)(2,1)S(1)}, bf16[512,2048]{1,0:T(8,128)(2,1)S(1)}, u32[]{:S(2)}, u32[]{:S(2)}) collective-permute-start(bf16[512,2048]{1,0:T(8,128)(2,1)S(1)} %pad_maximum_fusion.4), channel_id=1, source_target_pairs={{0,4},{4,0},{8,12},{12,8},{16,20},{20,16},{24,28},{28,24},{1,5},{5... | collective-permute-start | bytes 6291464 | tf_op jit(solution)/shard_map/ppermute | solution.py:42
  480.5 12.9 %slice-start = ((s8[16777216]{0:T(1024)(128)(4,1)}), s8[4194304]{0:T(1024)(128)(4,1)S(1)}, s32[]{:S(2)}) async-start(s8[16777216]{0:T(1024)(128)(4,1)} %bitcast.174), calls=%async_computation.12 | async-start | bytes 8388608
  480.5 12.9 %slice-start.1 = ((s8[16777216]{0:T(1024)(128)(4,1)}), s8[4194304]{0:T(1024)(128)(4,1)S(1)}, s32[]{:S(2)}) async-start(s8[16777216]{0:T(1024)(128)(4,1)} %bitcast.174), calls=%async_computation.13 | async-start | bytes 8388608
  480.5 12.9 %slice-start.2 = ((s8[16777216]{0:T(1024)(128)(4,1)}), s8[4194304]{0:T(1024)(128)(4,1)S(1)}, s32[]{:S(2)}) async-start(s8[16777216]{0:T(1024)(128)(4,1)} %bitcast.174), calls=%async_computation.14 | async-start | bytes 8388608
  544.0 123.8 %reduce-scatter.8.cloned.1.call-start = ((), (), s32[]{:S(2)}) async-start(), calls=%async_computation.9 | async-start | bytes 3604480 | tf_op jit(solution)/shard_map/reduce_scatter | solution.py:263
  557.8 82.7 %collective-permute-start.34 = (bf16[512,2048]{1,0:T(8,128)(2,1)}, bf16[512,2048]{1,0:T(8,128)(2,1)}, u32[]{:S(2)}, u32[]{:S(2)}) collective-permute-start(bf16[512,2048]{1,0:T(8,128)(2,1)} %slice.277), channel_id=1, source_target_pairs={{0,4},{4,0},{8,12},{12,8},{16,20},{20,16},{24,28},{28,24},{1,5},{5... | collective-permute-start | bytes 6291464 | tf_op jit(solution)/shard_map/ppermute | solution.py:42
  631.4 99.9 %all-to-all-start = ((bf16[8,64,1920]{2,1,0:T(8,128)(2,1)}), bf16[8,64,1920]{2,1,0:T(8,128)(2,1)}, u32[]{:S(2)}, u32[]{:S(2)}) async-start(bf16[8,64,1920]{2,1,0:T(8,128)(2,1)} %concatenate.103), calls=%async_computation | async-start | bytes 3932160 | tf_op jit(solution)/shard_map/all_to_all | solution.py:275
  636.0 63.3 %reduce-scatter.6.cloned.1.call-start = ((), (), s32[]{:S(2)}) async-start(), calls=%async_computation.8 | async-start | bytes 1310720 | tf_op jit(solution)/shard_map/reduce_scatter | solution.py:264
  645.9 81.3 %copy-start.4 = (bf16[1,128,2048]{2,1,0:T(8,128)(2,1)S(1)}, bf16[1,128,2048]{2,1,0:T(8,128)(2,1)}, u32[]{:S(2)}) copy-start(bf16[1,128,2048]{2,1,0:T(8,128)(2,1)} %param.13) | copy-start | bytes 1572868
  645.9 83.0 %copy-start.12 = (f32[128,2048]{1,0:T(8,128)S(1)}, f32[128,2048]{1,0:T(8,128)}, u32[]{:S(2)}) copy-start(f32[128,2048]{1,0:T(8,128)} %get-tuple-element.23) | copy-start | bytes 3145732
  647.1 54.0 %collective-permute-start.35 = (bf16[128,2048]{1,0:T(8,128)(2,1)}, bf16[128,2048]{1,0:T(8,128)(2,1)S(1)}, u32[]{:S(2)}, u32[]{:S(2)}) collective-permute-start(bf16[128,2048]{1,0:T(8,128)(2,1)} %get-tuple-element.42), channel_id=1, source_target_pairs={{0,24},{4,28},{8,0},{12,4},{16,8},{20,12},{24,16},{28,20},{1,25},{... | collective-permute-start | bytes 1572872 | tf_op jit(solution)/shard_map/ppermute | solution.py:57
  651.0 50.1 %collective-permute-start.37 = (bf16[128,2048]{1,0:T(8,128)(2,1)}, bf16[128,2048]{1,0:T(8,128)(2,1)S(1)}, u32[]{:S(2)}, u32[]{:S(2)}) collective-permute-start(bf16[128,2048]{1,0:T(8,128)(2,1)} %get-tuple-element.43), channel_id=1, source_target_pairs={{0,8},{4,12},{8,16},{12,20},{16,24},{20,28},{24,0},{28,4},{1,9},{5... | collective-permute-start | bytes 1572872 | tf_op jit(solution)/shard_map/ppermute | solution.py:57
  651.0 76.2 %collective-permute-start.36 = (bf16[128,2048]{1,0:T(8,128)(2,1)}, bf16[128,2048]{1,0:T(8,128)(2,1)S(1)}, u32[]{:S(2)}, u32[]{:S(2)}) collective-permute-start(bf16[128,2048]{1,0:T(8,128)(2,1)} %get-tuple-element.44), channel_id=1, source_target_pairs={{0,16},{4,20},{8,24},{12,28},{16,0},{20,4},{24,8},{28,12},{1,17},{... | collective-permute-start | bytes 1572872 | tf_op jit(solution)/shard_map/ppermute | solution.py:57
  (43 other events, 227.1 us)
Sparse Core Ops, SparseCore 0:
  11.2 33.9 all-gather.14
  47.0 103.4 all-gather.6
  153.0 58.7 all-gather.10
  214.0 43.8 all-gather.8
  260.1 41.6 all-gather.12
  544.1 78.9 reduce-scatter.9
  626.1 41.7 reduce-scatter.7
  671.3 27.9 reduce-scatter.5
